TPU v7x, 128 devices: a whole 4x4x4 slice. The times are simulated.
128 devices in a mesh: sec: 4 (over x), fsdp: 32 (over y, z, core).
Axes of the slice: x: 4, y: 4, z: 4, core: 2. Of those that a mesh axis runs over, the one named last changes fastest.
Arguments:
- tokens: bfloat16 [32768, 2560], P(('sec', 'fsdp')), may hold values from -36 to 36
- pre_gain: float32 [2560], replicated, may hold values from 0.1 to 1.9
- w_z: bfloat16 [2560, 2560], P('fsdp'), may hold values from -0.125 to 0.125
- w_x: bfloat16 [2560, 2560], P('fsdp'), may hold values from -0.125 to 0.125
- w_bc: bfloat16 [2560, 256], P('fsdp'), may hold values from -0.125 to 0.125
- w_dt: bfloat16 [2560, 40], P('fsdp'), may hold values from -0.125 to 0.125
- conv_weight: float32 [4, 2816], replicated, may hold values from -0.5 to 0.5
- conv_bias: float32 [2816], replicated, may hold values from -0.5 to 0.5
- dt_bias: float32 [40], replicated, may hold values from -9 to -2
- a_log: float32 [40], replicated, may hold values from -8 to 0
- d_skip: float32 [40], replicated, may hold values from 0.5 to 1.5
- norm_gain: float32 [2560], replicated, may hold values from 0.1 to 1.9
Outputs:
- mixed: bfloat16 [32768, 2560], P(('sec', 'fsdp'))
All inputs are finite; a program needn't handle non-finite values.
Results may differ from a plain program's by a relative error of at most 0.015.
Values may be sent and summed in bfloat16 or wider, within the bound.
A program may use at most 384 MiB of HBM per device.

v0:
```python
import jax
import jax.numpy as jnp
from jax import lax
from jax.sharding import Mesh
from jax.sharding import PartitionSpec as P

HEADDIM = 64
SPAN = 256
FSDP = ("fsdp_0", "fsdp_1", "fsdp_2")
SEC_FSDP = ("sec", "fsdp_0", "fsdp_1", "fsdp_2")


EPS = 1e-05


def in_one_piece(arrays, axis, dim, along):
    both = jnp.concatenate(arrays, axis=along)
    whole, at, done = (lax.all_gather(both, axis, axis=dim, tiled=True), 0, [])
    for a in arrays:
        done.append(lax.slice_in_dim(whole, at, at + a.shape[along], axis=along))
        at += a.shape[along]
    return tuple(done)


def shifted(value, axis, steps):
    count = lax.axis_size(axis)
    first, last = (max(0, -steps), min(count, count - steps))
    return lax.ppermute(value, axis, [(source, source + steps) for source in range(first, last)])


def neutral_like(shard, identity):
    return jax.tree.map(
        lambda a, e: jnp.broadcast_to(jnp.asarray(e, a.dtype), a.shape), shard, identity
    )


def entering(shard, axes, combine, identity):
    before = start = neutral_like(shard, identity)
    running = shard
    for axis in reversed(axes):
        peers, mine = (lax.axis_size(axis), lax.axis_index(axis))
        pieces = jax.tree.map(lambda part: lax.all_gather(part, axis), running)
        inside, running = (start, start)
        for k in range(peers):
            passed = k < mine
            running = combine(running, jax.tree.map(lambda part: part[k], pieces))
            inside = jax.tree.map(lambda new, old: jnp.where(passed, new, old), running, inside)
        before = combine(inside, before)
    return before


def rms_scale(values, gain_vec):
    mean_square = jnp.mean(values * values, axis=-1, keepdims=True)
    return values * lax.rsqrt(mean_square + EPS) * gain_vec


def causal_conv(stacked, kernel, offset_bias):
    kernel_len = kernel.shape[0]
    length = stacked.shape[0] - kernel_len + 1
    summed = offset_bias[None, :]
    for offset in range(kernel_len):
        summed = summed + kernel[offset][None, :] * stacked[offset : offset + length].astype(
            jnp.float32
        )
    return jax.nn.silu(summed).astype(jnp.bfloat16)


def block_terms(x_conv, b_conv, c_conv, step_dt, head_rates):
    length = step_dt.shape[1]
    cumulative = jnp.cumsum(step_dt * head_rates, axis=1)
    cum_heads = jnp.swapaxes(cumulative, 1, 2)
    dt_heads = jnp.swapaxes(step_dt, 1, 2)
    inner_dots = jnp.einsum("kqn,ksn->kqs", c_conv, b_conv, preferred_element_type=jnp.float32)
    causal = lax.broadcasted_iota(jnp.int32, (length, length), 0) >= lax.broadcasted_iota(
        jnp.int32, (length, length), 1
    )
    cum_gap = cum_heads[:, :, :, None] - cum_heads[:, :, None, :]
    decays = jnp.where(causal, jnp.exp(-jnp.where(causal, cum_gap, 0.0)), 0.0)
    scores = (decays * dt_heads[:, :, None, :] * inner_dots[:, None, :, :]).astype(jnp.bfloat16)
    y_intra = jnp.einsum("khqs,kshp->kqhp", scores, x_conv, preferred_element_type=jnp.float32)
    to_end = jnp.exp(-(cumulative[:, -1:, :] - cumulative)) * step_dt
    weighted = (x_conv.astype(jnp.float32) * to_end[..., None]).astype(jnp.bfloat16)
    block_state = jnp.einsum("kshp,ksn->khpn", weighted, b_conv, preferred_element_type=jnp.float32)
    return (y_intra, block_state, cumulative)


def state_output(c_conv, starts, cumulative):
    reached = jnp.einsum("kqn,khpn->kqhp", c_conv.astype(jnp.float32), starts)
    return reached * jnp.exp(-cumulative)[..., None]


def join_carry(earlier, latter):
    return (earlier[0] * latter[0], earlier[1] * latter[0][:, None, None] + latter[1])


def per_device(
    tokens,
    pre_gain,
    w_z,
    w_x,
    w_bc,
    w_dt,
    conv_weight,
    conv_bias,
    dt_bias,
    a_log,
    d_skip,
    norm_gain,
):
    tok_rows = tokens.shape[0]
    normed = rms_scale(tokens.astype(jnp.float32), pre_gain).astype(jnp.bfloat16)
    pieces = in_one_piece((w_z, w_x, w_bc, w_dt), FSDP, 0, 1)
    summed = tuple(
        (jnp.dot(normed, pieces[slot], preferred_element_type=jnp.float32) for slot in range(4))
    )
    z_part, x_part, bc_part, dt_raw = [partial_sum.astype(jnp.bfloat16) for partial_sum in summed]
    margin = conv_weight.shape[0] - 1
    tail_x, tail_bc = shifted(
        (x_part[tok_rows - margin :], bc_part[tok_rows - margin :]), SEC_FSDP, 1
    )
    inner_width = x_part.shape[1]
    x_conv = causal_conv(
        jnp.concatenate([tail_x, x_part], 0), conv_weight[:, :inner_width], conv_bias[:inner_width]
    )
    bc_conv = causal_conv(
        jnp.concatenate([tail_bc, bc_part], 0),
        conv_weight[:, inner_width:],
        conv_bias[inner_width:],
    )
    state_width = bc_conv.shape[1] // 2
    step_dt = jax.nn.softplus(dt_raw.astype(jnp.float32) + dt_bias)
    head_rates = jnp.exp(a_log)
    head_count = a_log.shape[0]
    blocks = tok_rows // SPAN
    x_blocks = x_conv.reshape(blocks, SPAN, head_count, HEADDIM)
    b_blocks = bc_conv[:, :state_width].reshape(blocks, SPAN, state_width)
    c_blocks = bc_conv[:, state_width:].reshape(blocks, SPAN, state_width)
    dt_blocks = step_dt.reshape(blocks, SPAN, head_count)
    y_intra, block_state, cumulative = block_terms(
        x_blocks, b_blocks, c_blocks, dt_blocks, head_rates
    )
    block_decay = jnp.exp(-cumulative[:, -1, :])
    running = jnp.zeros((head_count, HEADDIM, state_width), jnp.float32)
    start_list = [running]
    running = running * block_decay[0][:, None, None] + block_state[0]
    local_starts = jnp.stack(start_list, 0)
    total_decay = jnp.prod(block_decay, axis=0)
    identity = (jnp.ones_like(total_decay), jnp.zeros_like(running))
    incoming = entering((total_decay, running), SEC_FSDP, join_carry, identity)
    decay_before = jnp.cumprod(
        jnp.concatenate([jnp.ones((1, head_count), jnp.float32), block_decay[:-1]], 0), axis=0
    )
    starts = local_starts + decay_before[:, :, None, None] * incoming[1][None]
    y_state = state_output(c_blocks, starts, cumulative)
    y_total = (y_intra + y_state).reshape(tok_rows, inner_width) + jnp.repeat(d_skip, HEADDIM)[
        None, :
    ] * x_conv.astype(jnp.float32)
    gated = y_total * jax.nn.silu(z_part.astype(jnp.float32))
    return rms_scale(gated, norm_gain).astype(jnp.bfloat16)


def solution(mesh):
    torus = Mesh(
        mesh.devices.reshape(mesh.shape["sec"], 4, 4, 2), ("sec", "fsdp_0", "fsdp_1", "fsdp_2")
    )
    return jax.shard_map(
        per_device,
        mesh=torus,
        in_specs=(
            P(SEC_FSDP, None),
            P(),
            P(FSDP, None),
            P(FSDP, None),
            P(FSDP, None),
            P(FSDP, None),
            P(),
            P(),
            P(),
            P(),
            P(),
            P(),
        ),
        out_specs=P(SEC_FSDP, None),
        check_vma=False,
    )
```

profile of v0, /device:TPU:1, one launch (start us, length us, event | category | flops | bytes accessed | tf_op | source)
XLA Modules:
  0.0 379.5 jit_solution(15506762499310206582)
XLA Ops:
  7.4 2.2 pad_maximum_fusion.1
  10.2 103.0 %all-gather.11.cloned.1.call-done = bf16[2560,5416]{1,0:T(8,128)(2,1)} async-done(((bf16[80,5416]{1,0:T(8,128)(2,1)}), bf16[2560,5416]{1,0:T(8,128)(2,1)}) %all-gather.11.cloned.1.call-update) | async-done | bytes 27729936 | tf_op jit(solution)/shard_map/all_gather | solution.py:18
  116.0 1.9 fusion.60
  117.9 2.5 collective-permute-start.1
  120.4 9.4 %fusion.11 = bf16[256,2560]{1,0:T(8,128)(2,1)} fusion(bf16[2560,5416]{1,0:T(8,128)(2,1)} %all-gather.11.cloned.1.call-done, bf16[256,2560]{1,0:T(8,128)(2,1)S(1)} %copy-done.2, f32[2560]{0:T(1024)S(1)} %copy-done.9, f32[256]{0:T(256)S(1)} %add_rsqrt_fusion.1), kind=kOutput, calls=%fused_computation.12 | convolution fusion | flops 3358720000 | bytes 15739904 | tf_op jit(solution)/shard_map/dot_general | solution.py:114
  129.9 1.8 mul.549
  131.7 2.1 copy.49
  134.7 2.2 collective-permute-start
  137.7 5.3 %fusion.23 = (bf16[256,2560]{1,0:T(8,128)(2,1)}, bf16[256,2560]{1,0:T(8,128)(2,1)}) fusion(f32[256,2560]{1,0:T(8,128)S(1)} %copy.49, bf16[256,2560]{1,0:T(8,128)(2,1)} %fusion.11, f32[2560]{0:T(1024)S(1)} %get-tuple-element.6, bf16[3,2560]{1,0:T(4,128)(2,1)S(1)} %collective-permute-done, f32[2560]{0:T(1024)S(1)} %get-tuple-element.7, ...), kind=kLoop, calls=%fused_computation.22 | loop fusion | flops 19005440 | bytes 6620160 | tf_op jit(solution)/shard_map/convert_element_type | solution.py:82
  146.3 1.8 all-gather
  148.1 14.8 %all-gather.19.cloned.1.call-done = f32[80,64,128]{2,1,0:T(8,128)} async-done(((f32[40,64,128]{2,1,0:T(8,128)}), f32[80,64,128]{2,1,0:T(8,128)}) %all-gather.19.cloned.1.call-update) | async-done | bytes 2621456 | tf_op jit(solution)/shard_map/all_gather | solution.py:42
  162.9 3.0 fusion.36
  166.0 8.0 %all-gather.2 = f32[4,1,40]{2,1,0:T(1,128)S(1)} all-gather(f32[1,1,40]{2,1,0:T(1,128)S(1)} %get-tuple-element.34), channel_id=4, replica_groups=mesh['sec'=4,'fsdp_0'=4,'fsdp_1'=4,'fsdp_2'=2] {'fsdp_1'}, dimensions={0}, use_global_device_ids=true | all-gather | bytes 800 | tf_op jit(solution)/shard_map/all_gather | solution.py:42
  174.0 50.0 %all-gather.13.cloned.1.call-done = f32[4,40,64,128]{3,2,1,0:T(8,128)} async-done(((f32[1,40,64,128]{3,2,1,0:T(8,128)}), f32[4,40,64,128]{3,2,1,0:T(8,128)}) %all-gather.13.cloned.1.call-update) | async-done | bytes 5242896 | tf_op jit(solution)/shard_map/all_gather | solution.py:42
  224.0 4.0 %slice_add_fusion.8 = f32[1,40,64,128]{3,2,1,0:T(8,128)} fusion(f32[4,40,64,128]{3,2,1,0:T(8,128)} %all-gather.13.cloned.1.call-done, f32[40]{0:T(128)S(1)} %get-tuple-element.31, f32[40]{0:T(128)S(1)} %get-tuple-element.32, f32[40]{0:T(128)S(1)} %get-tuple-element.33, f32[40]{0:T(128)S(1)} %bitcast_multiply_fusion.4), kind=kLoop, calls=%fused_computation.47 | loop fusion | flops 2293760 | bytes 6554240 | tf_op jit(solution)/shard_map/add | solution.py:93
  228.0 7.7 %all-gather.3 = f32[4,1,40]{2,1,0:T(1,128)S(1)} all-gather(f32[1,1,40]{2,1,0:T(1,128)S(1)} %get-tuple-element.30), channel_id=1, replica_groups=mesh['sec'=4,'fsdp_0'=4,'fsdp_1'=4,'fsdp_2'=2] {'fsdp_0'}, dimensions={0}, use_global_device_ids=true | all-gather | bytes 800 | tf_op jit(solution)/shard_map/all_gather | solution.py:42
  235.7 49.7 %all-gather.15.cloned.1.call-done = f32[4,40,64,128]{3,2,1,0:T(8,128)} async-done(((f32[1,40,64,128]{3,2,1,0:T(8,128)}), f32[4,40,64,128]{3,2,1,0:T(8,128)}) %all-gather.15.cloned.1.call-update) | async-done | bytes 5242896 | tf_op jit(solution)/shard_map/all_gather | solution.py:42
  285.4 4.0 %slice_add_fusion.4 = f32[1,40,64,128]{3,2,1,0:T(8,128)} fusion(f32[4,40,64,128]{3,2,1,0:T(8,128)} %all-gather.15.cloned.1.call-done, f32[40]{0:T(128)S(1)} %get-tuple-element.27, f32[40]{0:T(128)S(1)} %get-tuple-element.28, f32[40]{0:T(128)S(1)} %get-tuple-element.29, f32[40]{0:T(128)S(1)} %bitcast_multiply_fusion.6), kind=kLoop, calls=%fused_computation.43 | loop fusion | flops 2293760 | bytes 6554240 | tf_op jit(solution)/shard_map/add | solution.py:93
  290.5 7.8 %all-gather.4 = f32[4,1,40]{2,1,0:T(1,128)S(1)} all-gather(f32[1,1,40]{2,1,0:T(1,128)S(1)} %get-tuple-element.26), channel_id=1, replica_groups=mesh['sec'=4,'fsdp_0'=4,'fsdp_1'=4,'fsdp_2'=2] {'sec'}, dimensions={0}, use_global_device_ids=true | all-gather | bytes 800 | tf_op jit(solution)/shard_map/all_gather | solution.py:42
  300.0 46.9 %all-gather.17.cloned.1.call-done = f32[4,40,64,128]{3,2,1,0:T(8,128)} async-done(((f32[1,40,64,128]{3,2,1,0:T(8,128)}), f32[4,40,64,128]{3,2,1,0:T(8,128)}) %all-gather.17.cloned.1.call-update) | async-done | bytes 5242896 | tf_op jit(solution)/shard_map/all_gather | solution.py:42
  346.9 6.4 %fusion.34 = f32[256,40,64]{0,2,1:T(8,128)S(1)} fusion(f32[4,40,64,128]{3,2,1,0:T(8,128)} %all-gather.17.cloned.1.call-done, f32[1,40,64,128]{3,2,1,0:T(8,128)S(1)} %copy-done.1, f32[1,40,64,128]{3,2,1,0:T(8,128)} %slice_add_fusion.8, f32[1,40,64,128]{3,2,1,0:T(8,128)} %slice_add_fusion.4, f32[4,40,64,128]{3,2,1,0:T(8,128)} %all-gather.13.cloned.1.call-done, ...), kind=kOutput, calls=%fused_computation.39 | convolution fusion | flops 180224000 | bytes 21044238 | tf_op jit(solution)/shard_map/kqn,khpn->kqhp/dot_general | solution.py:88
  353.4 5.2 %bitcast_add_fusion = f32[1,256,40,64]{1,3,2,0:T(8,128)} fusion(f32[256,40,64]{0,2,1:T(8,128)S(1)} %fusion.34, bf16[256,40,64]{0,2,1:T(8,128)(2,1)S(1)} %bitcast.140, f32[256,256]{1,0:T(8,128)S(1)} %fusion.102, f32[40,256]{1,0:T(8,128)S(1)} %copy.46, f32[40,256]{1,0:T(8,128)S(1)} %bitcast_add_fusion.2, pred[256,256]{1,0:T(8,128)(4,1)S(1)} %iota_compare_fusion, ...), kind=kOutput, calls=%fused_computation.25 | convolution fusion | flops 355205120 | bytes 7004160 | tf_op jit(solution)/shard_map/khqs,kshp->kqhp/dot_general | solution.py:80
  358.6 3.4 copy.52
  362.0 9.6 %multiply_reduce_fusion = (f32[256]{0:T(256)S(1)}, f32[256,2560]{1,0:T(8,128)S(1)}) fusion(bf16[2560,5416]{1,0:T(8,128)(2,1)} %all-gather.11.cloned.1.call-done, bf16[256,2560]{1,0:T(8,128)(2,1)S(1)} %copy-done.3, f32[2560]{0:T(1024)S(1)} %copy-done.9, f32[256]{0:T(256)S(1)} %add_rsqrt_fusion.1, f32[256,2560]{1,0:T(8,128)} %copy.52, ...), kind=kOutput, calls=%fused_computation.27 | convolution fusion | flops 3365928704 | bytes 20994048 | tf_op jit(solution)/shard_map/dot_general | solution.py:114
  (81 shorter events, 13.3 us)
Async XLA Ops:
  6.5 106.7 %all-gather.11.cloned.1.call-start = ((), (), s32[]{:S(2)}) async-start(), calls=%async_computation | async-start | bytes 29061120 | tf_op jit(solution)/shard_map/all_gather | solution.py:18
  7.3 2.4 copy-start.10
  7.3 2.4 copy-start.6
  7.4 2.4 copy-start.5
  7.4 2.5 copy-start.2
  9.6 103.6 %copy-start.9 = (f32[2560]{0:T(1024)S(1)}, f32[2560]{0:T(1024)}, u32[]{:S(2)}) copy-start(f32[2560]{0:T(1024)} %param.13) | copy-start | bytes 30724
  9.6 103.6 %copy-start.11 = (f32[40]{0:T(128)S(1)}, f32[40]{0:T(128)}, u32[]{:S(2)}) copy-start(f32[40]{0:T(128)} %param.20) | copy-start | bytes 484
  9.6 153.3 %all-gather.19.cloned.1.call-start = ((), (), s32[]{:S(2)}) async-start(), calls=%async_computation.4 | async-start | bytes 3932160 | tf_op jit(solution)/shard_map/all_gather | solution.py:42
  117.9 18.9 %collective-permute-start.1 = (bf16[3,256]{1,0:T(4,128)(2,1)S(1)}, bf16[3,256]{1,0:T(4,128)(2,1)S(1)}, u32[]{:S(2)}, u32[]{:S(2)}) collective-permute-start(bf16[3,256]{1,0:T(4,128)(2,1)S(1)} %slice.256), channel_id=1, source_target_pairs={{0,1},{1,2},{2,3},{3,4},{4,5},{5,6},{6,7},{7,8},{8,9},{9,10},{10,1... | collective-permute-start | bytes 4616 | tf_op jit(solution)/shard_map/ppermute | solution.py:28
  134.7 3.1 collective-permute-start
  146.2 77.7 %all-gather.13.cloned.1.call-start = ((), (), s32[]{:S(2)}) async-start(), calls=%async_computation.1 | async-start | bytes 6553600 | tf_op jit(solution)/shard_map/all_gather | solution.py:42
  165.9 119.5 %all-gather.15.cloned.1.call-start = ((), (), s32[]{:S(2)}) async-start(), calls=%async_computation.2 | async-start | bytes 6553600 | tf_op jit(solution)/shard_map/all_gather | solution.py:42
  228.0 119.0 %all-gather.17.cloned.1.call-start = ((), (), s32[]{:S(2)}) async-start(), calls=%async_computation.3 | async-start | bytes 6553600 | tf_op jit(solution)/shard_map/all_gather | solution.py:42
  289.4 0.7 copy-start.8
  289.4 9.1 %copy-start = (bf16[256,2560]{1,0:T(8,128)(2,1)S(1)}, bf16[256,2560]{1,0:T(8,128)(2,1)}, u32[]{:S(2)}) copy-start(bf16[256,2560]{1,0:T(8,128)(2,1)} %get-tuple-element.15) | copy-start | bytes 3932164
  298.5 48.4 %copy-start.1 = (f32[1,40,64,128]{3,2,1,0:T(8,128)S(1)}, f32[1,40,64,128]{3,2,1,0:T(8,128)}, u32[]{:S(2)}) copy-start(f32[1,40,64,128]{3,2,1,0:T(8,128)} %fusion.36) | copy-start | bytes 3932164
  346.9 6.4 %copy-start.4 = (bf16[256,2560]{0,1:T(8,128)(2,1)S(1)}, bf16[256,2560]{0,1:T(8,128)(2,1)}, u32[]{:S(2)}) copy-start(bf16[256,2560]{0,1:T(8,128)(2,1)} %copy.41) | copy-start | bytes 3932164
  358.6 3.4 copy-start.3
  362.0 9.6 %copy-start.7 = (f32[2560]{0:T(1024)S(1)}, f32[2560]{0:T(1024)}, u32[]{:S(2)}) copy-start(f32[2560]{0:T(1024)} %param.23) | copy-start | bytes 30724
Sparse Core Ops, SparseCore 0:
  9.8 103.4 all-gather.10
  146.3 16.4 all-gather.18
  166.0 57.8 all-gather.12
  228.1 57.2 all-gather.14
  289.5 57.3 all-gather.16
where the time goes:
time: 380 us; the launch traced here: 379 us
  waiting for transfers between devices  265 us (70%)
  matrix products  35.9 us (9%)
  blocking collectives  25.3 us (7%)
  other arithmetic  21.2 us (6%)
  local copies, waits for them, and re-layouts  13.6 us (4%)
  between operations  13.5 us (4%)
  starting transfers between devices  4.84 us (1%)
    all_gather x4, waiting for transfers between devices, entering(): pieces = jax.tree.map(lambda part: lax.all_gather(part, axis), running)  161 us
    all_gather x1, waiting for transfers between devices, in_one_piece(): whole, at, done = (lax.all_gather(both, axis, axis=dim, tiled=True), 0, [])  103 us
    all_gather x4, blocking collectives, entering(): pieces = jax.tree.map(lambda part: lax.all_gather(part, axis), running)  25.3 us
    dot_general x4, matrix products, per_device(): jnp.dot(normed, pieces[slot], preferred_element_type=jnp.float32)  22.5 us
    add x3, other arithmetic, join_carry(): earlier[1] * latter[0][:, None, None] + latter[1]  11 us
  transfers between devices with their start and end apart: 7, of which 6 were waited for; matrix products, arithmetic and copies ran while one was open for 4% of the time, Pallas kernels for 0%

commit v1 on v0

v1 whole, which is shorter than its diff:
```python
import functools

import jax
import jax.numpy as jnp
from jax import lax
from jax.experimental import pallas as pl
from jax.experimental.pallas import tpu as pltpu
from jax.sharding import Mesh
from jax.sharding import PartitionSpec as P

AXES = ("sec", "fy", "fz", "fc")
FSDP = AXES[1:]
MESH = pl.DeviceIdType.MESH
F32, BF16 = jnp.float32, jnp.bfloat16

MODEL = 2560
HALF = 1280
STATE = 128
HEADDIM = 64
HALF_HEADS = 20
TOKENS = 256
CHIP_TOKENS = 512
HALO = 16
CHUNK = 128
CHUNKS = 4
SHARD = 80
FIRST = HALF + 2 * STATE
EPS = 1e-05
LOG2E = 1.4426950408889634
SPLIT = 48

N_GATHER = 2 * 2 * (2 + 2 + 8 + 6)
N_EDGE = 16


def dot(a, b, **kw):
    return jnp.dot(a, b, preferred_element_type=F32, **kw)


def contract(a, b, da, db):
    return lax.dot_general(a, b, (((da,), (db,)), ((), ())), preferred_element_type=F32)


def aligned(i, n):
    return pl.multiple_of(i, n)


class Gather:
    def __init__(self, w, sends, recvs, base, where):
        self.w, self.sends, self.recvs, self.next = w, sends, recvs, base
        self.x, self.y, self.z, self.c = where
        self.all = []
        self.m = {}
        for s in (0, 1):
            for sign in (1, -1):
                self.add("p1", s, sign, 0, 0, 0)
                lo, hi = (0, SPLIT) if sign == 1 else (SPLIT, SHARD)
                self.add("f1", s, sign, 0, -sign, 0, lo, hi)
                for o in (0, -1, 1, 2):
                    self.add("p2", s, sign, 1, o, 0)
            self.add("f2", s, 1, 1, 0, -1)
            self.add("f2", s, -1, 1, 1, 1)
            self.add("f2", s, 1, 1, -1, -1, 0, SHARD - SPLIT)
            self.add("f2", s, -1, 1, -1, 1, SHARD - SPLIT, SHARD)
            self.add("f2", s, 1, 1, 2, -1, 0, SPLIT)
            self.add("f2", s, -1, 1, 2, 1, SPLIT, SHARD)

    def rows(self, s, o1, o2, lo, hi):
        oy, oz = (o1, o2) if s == 0 else (o2, o1)
        yy, zz = (self.y + (oy + 4)) % 4, (self.z + (oz + 4)) % 4
        start = (yy * 4 + zz) * (2 * SHARD) + (s * SHARD + lo)
        return self.w.at[pl.ds(aligned(start, 16), hi - lo), :]

    def add(self, kind, s, sign, which, o1, o2, lo=0, hi=SHARD):
        along_y = (which == 0) == (s == 0)
        if along_y:
            dev = (self.x, (self.y + (sign + 4)) % 4, self.z, self.c)
        else:
            dev = (self.x, self.y, (self.z + (sign + 4)) % 4, self.c)
        k = self.next
        self.next += 1
        src = self.rows(s, o1, o2, lo, hi)
        r1, r2 = (o1 - sign, o2) if which == 0 else (o1, o2 - sign)
        land = self.rows(s, r1, r2, lo, hi)
        out = pltpu.make_async_remote_copy(src, src, self.sends.at[k], self.recvs.at[k], device_id=dev, device_id_type=MESH)
        back = pltpu.make_async_remote_copy(land, land, self.sends.at[k], self.recvs.at[k], device_id=dev, device_id_type=MESH)
        self.m[kind, s, sign, o1] = (out, back)
        self.all.append(out)

    def go(self, *key):
        self.m[key][0].start()

    def got(self, *key):
        self.m[key][1].wait_recv()

    def begin(self):
        for s in (0, 1):
            self.go("p1", s, 1, 0)
            self.go("p1", s, -1, 0)
        for s in (0, 1):
            self.go("p2", s, 1, 0)
            self.go("p2", s, -1, 0)

    def service(self, step):
        for s in (0, 1):
            if step == 0:
                self.got("p1", s, 1, 0)
                self.go("f1", s, 1, -1)
                self.go("p2", s, 1, -1)
                self.go("p2", s, -1, -1)
            elif step == 1:
                self.got("p1", s, -1, 0)
                self.go("f1", s, -1, 1)
                self.go("p2", s, 1, 1)
                self.go("p2", s, -1, 1)
            elif step == 2:
                self.got("p2", s, 1, 0)
                self.go("f2", s, 1, 0)
                self.got("p2", s, -1, 0)
            elif step == 3:
                self.got("f1", s, 1, -1)
                self.got("f1", s, -1, 1)
                self.go("p2", s, 1, 2)
                self.go("p2", s, -1, 2)
            elif step == 4:
                self.got("p2", s, 1, -1)
                self.go("f2", s, 1, -1)
                self.got("p2", s, -1, -1)
                self.go("f2", s, -1, -1)
            elif step == 5:
                self.got("p2", s, 1, 1)
                self.got("p2", s, -1, 1)
                self.go("f2", s, -1, 1)
            elif step == 6:
                self.got("p2", s, 1, 2)
                self.go("f2", s, 1, 2)
                self.got("p2", s, -1, 2)
                self.go("f2", s, -1, 2)
            else:
                for sign, o in ((1, 0), (-1, 1), (1, -1), (-1, -1), (1, 2), (-1, 2)):
                    self.got("f2", s, sign, o)

    def drain(self):
        for out in self.all:
            out.wait_send()


def silu(v):
    return v / (1.0 + jnp.exp(-v))


def kernel(
    tok, par, wx, wz, wbc, wdt, out,
    w1, w2, nt, pre, xc, bc, y, stl, sbuf, rbuf, pbuf, st0, st0f,
    dts, cum, row, e2, tmp, dec, dsk, cs, cr, drow, pfx, xt, xtr, xcs, xcr,
    gs, gr, ss, sss, ssr,
    local_sem, gsend, grecv, esend, erecv, asend, arecv, csend, crecv, bsend, brecv, xsend, xrecv,
):
    x, yy, zz, c = [lax.axis_index(a) for a in AXES]
    plane = yy * 4 + zz
    chip = x * 16 + plane
    sib = (x, yy, zz, 1 - c)

    def chip_dev(s):
        return (s // 16, (s // 4) % 4, s % 4, c)

    def plane_dev(q):
        return (x, q // 4, q % 4, c)

    after, before = (chip + 1) % 64, (chip + 63) % 64

    def remote(src, dst, send, recv, dev):
        return pltpu.make_async_remote_copy(src, dst, send, recv, device_id=dev, device_id_type=MESH)

    barrier = pltpu.get_barrier_semaphore()
    targets = [sib, chip_dev(after), chip_dev(before)]
    targets += [plane_dev((plane + o) % 16) for o in range(1, 16)]
    targets += [((x + o) % 4, yy, zz, c) for o in range(1, 4)]
    for dev in targets:
        pl.semaphore_signal(barrier, inc=1, device_id=dev, device_id_type=MESH)

    mine = pl.ds(aligned((plane * 2 + c) * SHARD, 16), SHARD)
    lane_c = pl.ds(aligned(c * HALF, 128), HALF)
    lane_o = pl.ds(aligned((1 - c) * HALF, 128), HALF)
    bc_c = pl.ds(aligned(c * STATE, 128), STATE)
    bc_o = pl.ds(aligned((1 - c) * STATE, 128), STATE)
    places = ((w1, 0, HALF), (w1, HALF, STATE), (w1, HALF + STATE, STATE), (w2, 0, HALF))
    own = (wx.at[:, lane_c], wbc.at[:, bc_c], wdt, wz.at[:, lane_c])
    others = (wx.at[:, lane_o], wbc.at[:, bc_o], wdt, wz.at[:, lane_o])
    locals_ = [
        pltpu.make_async_copy(src, w.at[mine, pl.ds(at, n)], local_sem.at[k])
        for k, (src, (w, at, n)) in enumerate(zip(own, places))
    ]
    gives = [
        remote(src, w.at[mine, pl.ds(at, n)], esend.at[k], erecv.at[k], sib)
        for k, (src, (w, at, n)) in enumerate(zip(others, places))
    ]
    for copy in locals_:
        copy.start()

    base_rows = aligned(HALO + c * TOKENS, 16)
    gain = par[5:6, 0:MODEL]

    def normalize(r, carry):
        v = tok[pl.ds(aligned(r * 32, 32), 32), :].astype(F32)
        mean = jnp.mean(v * v, axis=-1, keepdims=True)
        nt[pl.ds(aligned(base_rows + r * 32, 16), 32), :] = (v * lax.rsqrt(mean + EPS) * gain).astype(BF16)
        return carry

    pl.semaphore_wait(barrier, len(targets))
    for copy in gives:
        copy.start()
    lax.fori_loop(0, TOKENS // 32, normalize, 0)
    tok_rows = nt.at[pl.ds(base_rows, TOKENS), :]
    swap = remote(tok_rows, tok_rows, esend.at[4], erecv.at[4], sib)
    swap.start()

    where = (x, yy, zz, c)
    g1 = Gather(w1, gsend, grecv, 0, where)
    g2 = Gather(w2, gsend, grecv, N_GATHER // 2, where)
    for k in range(3):
        locals_[k].wait()
        gives[k].wait_recv()
    g1.begin()

    kk = lax.broadcasted_iota(jnp.int32, (2 * STATE, 256), 0) % STATE
    for j in range(HALF // 256):
        ll = (lax.broadcasted_iota(jnp.int32, (2 * STATE, 256), 1) + j * 256) // HEADDIM
        e2[:, j * 256 : (j + 1) * 256] = jnp.where(kk == ll, 1.0, 0.0).astype(BF16)

    def halves(v):
        hi = v.astype(BF16)
        lo = (v - hi.astype(F32)).astype(BF16)
        return jnp.concatenate([hi, lo], axis=1)

    roll_by = (STATE - HALF_HEADS * c) % STATE
    skip = pltpu.roll(jnp.broadcast_to(par[9:10, 0:STATE], (8, STATE)), roll_by, 1)
    dsk[...] = dot(halves(skip), e2[...])

    swap.wait_recv()
    halo_src, halo_dst = nt.at[pl.ds(CHIP_TOKENS, HALO), :], nt.at[pl.ds(0, HALO), :]
    halo = remote(halo_src, halo_dst, esend.at[5], erecv.at[5], chip_dev(after))
    halo.start()
    halo.wait_recv()

    @pl.when(chip == 0)
    def _():
        nt[0:HALO, :] = jnp.zeros((HALO, MODEL), BF16)

    for step in range(7):
        g1.service(step)
    locals_[3].wait()
    gives[3].wait_recv()
    g2.begin()
    g1.service(7)

    def project(j, carry):
        lanes = pl.ds(aligned(j * 256, 256), 256)
        pre[:, lanes] = dot(nt[...], w1[:, lanes])
        return carry

    lax.fori_loop(0, 3, project, 0)
    g2.service(0)
    lax.fori_loop(3, 6, project, 0)
    g2.service(1)

    rate = jnp.exp(par[8:9, 0:STATE]) * LOG2E
    bias = par[7:8, 0:STATE]
    tri = jnp.where(
        lax.broadcasted_iota(jnp.int32, (CHUNK, CHUNK), 0) >= lax.broadcasted_iota(jnp.int32, (CHUNK, CHUNK), 1), 1.0, 0.0
    )

    def steps(i, carry):
        rows = pl.ds(aligned(i * CHUNK, CHUNK), CHUNK)
        raw = pre[pl.ds(aligned(HALO + i * CHUNK, 16), CHUNK), HALF + STATE : FIRST] + bias
        dt = jnp.maximum(raw, 0.0) + jnp.log1p(jnp.exp(-jnp.abs(raw)))
        total = dot(tri, pltpu.roll(dt * rate, roll_by, 1), precision=lax.Precision.HIGHEST)
        dt = pltpu.roll(dt, roll_by, 1)
        dts[rows, :] = dt
        cum[rows, :] = total
        row[i] = (total + jnp.log(dt) * LOG2E).T
        return carry

    lax.fori_loop(0, CHUNKS, steps, 0)
    running = jnp.zeros((1, STATE), F32)
    for i in range(CHUNKS):
        last = cum[i * CHUNK + CHUNK - 1 : (i + 1) * CHUNK, :]
        tmp[i : i + 1, :] = last
        tmp[4 + i : 5 + i, :] = running
        running = running + last
    cs[...] = jnp.broadcast_to(running, (8, STATE))
    cr[plane] = jnp.broadcast_to(running, (8, STATE))
    totals, totals_in = [], []
    for o in range(1, 16):
        q, p = (plane + o) % 16, (plane + (16 - o)) % 16
        totals.append(remote(cs, cr.at[plane], csend.at[o - 1], crecv.at[o - 1], plane_dev(q)))
        totals_in.append(remote(cs, cr.at[p], csend.at[o - 1], crecv.at[o - 1], plane_dev(q)))
    for copy in totals:
        copy.start()
    dec[...] = dot(halves(jnp.exp2(-tmp[...])), e2[...])

    def convolve(at, col):
        taps = [par[k : k + 1, col] for k in range(4)]
        offset = par[4:5, col]
        parts = []
        for r in range(0, CHIP_TOKENS, CHUNK):
            v = offset
            for k in range(4):
                v = v + taps[k] * pre[HALO - 3 + k + r : HALO - 3 + k + r + CHUNK, at]
            parts.append(silu(v).astype(BF16))
        return parts

    bcs = convolve(pl.ds(HALF, STATE), pl.ds(aligned(2 * HALF + c * STATE, 128), STATE))
    for r, part in enumerate(bcs):
        bc[c, r * CHUNK : (r + 1) * CHUNK, :] = part
    swap_bc = remote(bc.at[c], bc.at[c], esend.at[6], erecv.at[6], sib)
    swap_bc.start()

    def conv_x(j, carry):
        at = pl.ds(aligned(j * 128, 128), 128)
        parts = convolve(at, pl.ds(aligned(c * HALF + j * 128, 128), 128))
        for r, part in enumerate(parts):
            xc[r * CHUNK : (r + 1) * CHUNK, at] = part
        return carry

    lax.fori_loop(0, HALF // 128, conv_x, 0)
    g2.service(2)
    swap_bc.wait_recv()

    stl[0] = jnp.zeros((STATE, HALF), F32)

    def states(i, carry):
        rows = pl.ds(aligned(i * CHUNK, CHUNK), CHUNK)
        to_end = halves(jnp.exp2(cum[rows, :] - tmp[pl.ds(i, 1), :]) * dts[rows, :])
        b = bc[0, rows, :]
        for j in range(HALF // 256):
            at = slice(j * 256, (j + 1) * 256)
            weighted = (dot(to_end, e2[:, at]) * xc[rows, at].astype(F32)).astype(BF16)
            stl[i + 1, :, at] = stl[i, :, at] * dec[pl.ds(i, 1), at] + contract(b, weighted, 0, 0)
        return carry

    lax.fori_loop(0, CHUNKS, states, 0)
    for q in range(16):
        sbuf[q] = stl[CHUNKS, q * 8 : (q + 1) * 8, :].astype(BF16)
    rbuf[plane] = sbuf[plane]
    parts_out, parts_in = [], []
    for o in range(1, 16):
        q, p = (plane + o) % 16, (plane + (16 - o)) % 16
        parts_out.append(remote(sbuf.at[q], rbuf.at[plane], asend.at[o - 1], arecv.at[o - 1], plane_dev(q)))
        parts_in.append(remote(sbuf.at[q], rbuf.at[p], asend.at[o - 1], arecv.at[o - 1], plane_dev(q)))
    for copy in parts_out:
        copy.start()
    g2.service(3)

    causal = lax.broadcasted_iota(jnp.int32, (CHUNK, CHUNK), 0) >= lax.broadcasted_iota(jnp.int32, (CHUNK, CHUNK), 1)
    low = jnp.where(lax.broadcasted_iota(jnp.int32, (CHUNK, 128), 1) < HEADDIM, 1.0, 0.0).astype(BF16)
    high = (1.0 - low.astype(F32)).astype(BF16)

    def intra(i, carry):
        rows = pl.ds(aligned(i * CHUNK, CHUNK), CHUNK)
        inner = contract(bc[1, rows, :], bc[0, rows, :], 1, 1)
        for pair in range(HALF_HEADS // 2):
            both = []
            for h in (2 * pair, 2 * pair + 1):
                gap = row[i, h : h + 1, :] - cum[rows, h : h + 1]
                both.append((jnp.exp2(jnp.where(causal, gap, -1e30)) * inner).astype(BF16))
            at = slice(pair * 128, (pair + 1) * 128)
            xp = xc[rows, at]
            spread = jnp.concatenate([xp * low, xp * high], axis=0)
            y[rows, at] = dot(jnp.concatenate(both, axis=1), spread) + dsk[0:1, at] * xp.astype(F32)
        return carry

    lax.fori_loop(0, 2, intra, 0)
    g2.service(4)
    lax.fori_loop(2, CHUNKS, intra, 0)

    for copy in totals_in:
        copy.wait_recv()
    for copy in parts_in:
        copy.wait_recv()
    drow[...] = dot(halves(jnp.exp2(-cr[:, 0, :])), e2[...])

    def prefix(k, state):
        pfx[k] = state
        return state * drow[pl.ds(k, 1), :] + rbuf[k].astype(F32)

    whole = lax.fori_loop(0, 16, prefix, jnp.zeros((8, HALF), F32))
    xt[...] = whole
    plane_total = jnp.zeros((8, STATE), F32)
    for k in range(16):
        plane_total = plane_total + cr[k]
    xcs[...] = plane_total
    sec_out, sec_in = [], []
    for o in range(1, 4):
        q, p = (x + o) % 4, (x + (4 - o)) % 4
        for k, (src, dst) in enumerate(((xt, xtr), (xcs, xcr))):
            n = 2 * (o - 1) + k
            sec_out.append(remote(src, dst.at[x], xsend.at[n], xrecv.at[n], (q, yy, zz, c)))
            sec_in.append(remote(src, dst.at[p], xsend.at[n], xrecv.at[n], (q, yy, zz, c)))
    for copy in sec_out:
        copy.start()
    xtr[x] = whole
    xcr[x] = plane_total
    g2.service(5)
    for copy in sec_in:
        copy.wait_recv()
    enter = jnp.zeros((8, HALF), F32)
    for k in range(3):
        moved = enter * dot(halves(jnp.exp2(-xcr[k])), e2[...]) + xtr[k]
        enter = jnp.where(k < x, moved, enter)

    def begin_states(k, state):
        pbuf[k] = (pfx[k] + state).astype(BF16)
        return state * drow[pl.ds(k, 1), :]

    lax.fori_loop(0, 16, begin_states, enter)
    st0[plane] = pbuf[plane]
    starts_out, starts_in = [], []
    for o in range(1, 16):
        q, p = (plane + o) % 16, (plane + (16 - o)) % 16
        starts_out.append(remote(pbuf.at[q], st0.at[plane], bsend.at[o - 1], brecv.at[o - 1], plane_dev(q)))
        starts_in.append(remote(pbuf.at[q], st0.at[p], bsend.at[o - 1], brecv.at[o - 1], plane_dev(q)))
    for copy in starts_out:
        copy.start()
    g2.service(6)
    for copy in starts_in:
        copy.wait_recv()
    for k in range(16):
        st0f[k * 8 : (k + 1) * 8, :] = st0[k].astype(F32)

    def carried(i, carry):
        rows = pl.ds(aligned(i * CHUNK, CHUNK), CHUNK)
        reach = halves(jnp.exp2(-cum[rows, :]))
        cc = bc[1, rows, :]
        for j in range(HALF // 256):
            at = slice(j * 256, (j + 1) * 256)
            state = (stl[i, :, at] + st0f[:, at] * dec[pl.ds(CHUNKS + i, 1), at]).astype(BF16)
            y[rows, at] = y[rows, at] + dot(cc, state) * dot(reach, e2[:, at])
        return carry

    lax.fori_loop(0, CHUNKS, carried, 0)
    g2.service(7)

    ss[...] = jnp.zeros((CHIP_TOKENS, 128), F32)
    theirs = pl.ds(aligned((1 - c) * TOKENS, TOKENS), TOKENS)
    ours = pl.ds(aligned(c * TOKENS, TOKENS), TOKENS)

    def gate(j, carry):
        at = pl.ds(aligned(j * 256, 256), 256)
        gated = y[:, at] * silu(dot(nt[HALO:, :], w2[:, at]))
        y[:, at] = gated
        square = gated * gated
        ss[...] = ss[...] + square[:, 0:128] + square[:, 128:256]
        gs[:, at] = y[theirs, at].astype(BF16)
        remote(gs.at[:, at], gr.at[:, at], esend.at[8 + j], erecv.at[8 + j], sib).start()
        return carry

    lax.fori_loop(0, HALF // 256, gate, 0)
    sss[...] = ss[theirs, :]
    sums = remote(sss, ssr, esend.at[7], erecv.at[7], sib)
    sums.start()
    sums.wait_recv()
    mean = jnp.sum(ss[ours, :] + ssr[...], axis=-1, keepdims=True) * (1.0 / MODEL)
    scale = lax.rsqrt(mean + EPS)
    for j in range(HALF // 256):
        at = slice(j * 256, (j + 1) * 256)
        spot = pl.ds(aligned(c * HALF + j * 256, 128), 256)
        out[:, spot] = (y[ours, at] * scale * par[6:7, spot]).astype(BF16)
    for j in range(HALF // 256):
        at = slice(j * 256, (j + 1) * 256)
        part = remote(gs.at[:, at], gr.at[:, at], esend.at[8 + j], erecv.at[8 + j], sib)
        part.wait_recv()
        spot = pl.ds(aligned((1 - c) * HALF + j * 256, 128), 256)
        out[:, spot] = (gr[:, at].astype(F32) * scale * par[6:7, spot]).astype(BF16)
        part.wait_send()

    g1.drain()
    g2.drain()
    for copy in gives + [swap, halo, swap_bc, sums] + totals + parts_out + sec_out + starts_out:
        copy.wait_send()


def per_device(
    tokens, pre_gain, w_z, w_x, w_bc, w_dt, conv_weight, conv_bias, dt_bias, a_log, d_skip, norm_gain
):
    width = conv_weight.shape[1]

    def line(v):
        return jnp.pad(v, (0, width - v.shape[0]))[None]

    par = jnp.concatenate(
        [conv_weight, line(conv_bias), line(pre_gain), line(norm_gain), line(dt_bias), line(a_log), line(d_skip)], 0
    )
    wdt = jnp.pad(w_dt, ((0, 0), (0, STATE - w_dt.shape[1])))
    vmem, anywhere = pl.BlockSpec(memory_space=pltpu.VMEM), pl.BlockSpec(memory_space=pl.ANY)
    dma = pltpu.SemaphoreType.DMA
    return pl.pallas_call(
        kernel,
        out_shape=jax.ShapeDtypeStruct((TOKENS, MODEL), BF16),
        in_specs=[vmem, vmem, anywhere, anywhere, anywhere, anywhere],
        out_specs=vmem,
        scratch_shapes=[
            pltpu.VMEM((MODEL, FIRST), BF16),
            pltpu.VMEM((MODEL, HALF), BF16),
            pltpu.VMEM((HALO + CHIP_TOKENS, MODEL), BF16),
            pltpu.VMEM((HALO + CHIP_TOKENS, FIRST), F32),
            pltpu.VMEM((CHIP_TOKENS, HALF), BF16),
            pltpu.VMEM((2, CHIP_TOKENS, STATE), BF16),
            pltpu.VMEM((CHIP_TOKENS, HALF), F32),
            pltpu.VMEM((CHUNKS + 1, STATE, HALF), F32),
            pltpu.VMEM((16, 8, HALF), BF16),
            pltpu.VMEM((16, 8, HALF), BF16),
            pltpu.VMEM((16, 8, HALF), BF16),
            pltpu.VMEM((16, 8, HALF), BF16),
            pltpu.VMEM((STATE, HALF), F32),
            pltpu.VMEM((CHIP_TOKENS, STATE), F32),
            pltpu.VMEM((CHIP_TOKENS, STATE), F32),
            pltpu.VMEM((CHUNKS, STATE, CHUNK), F32),
            pltpu.VMEM((2 * STATE, HALF), BF16),
            pltpu.VMEM((8, STATE), F32),
            pltpu.VMEM((8, HALF), F32),
            pltpu.VMEM((8, HALF), F32),
            pltpu.VMEM((8, STATE), F32),
            pltpu.VMEM((16, 8, STATE), F32),
            pltpu.VMEM((16, HALF), F32),
            pltpu.VMEM((16, 8, HALF), F32),
            pltpu.VMEM((8, HALF), F32),
            pltpu.VMEM((4, 8, HALF), F32),
            pltpu.VMEM((8, STATE), F32),
            pltpu.VMEM((4, 8, STATE), F32),
            pltpu.VMEM((TOKENS, HALF), BF16),
            pltpu.VMEM((TOKENS, HALF), BF16),
            pltpu.VMEM((CHIP_TOKENS, 128), F32),
            pltpu.VMEM((TOKENS, 128), F32),
            pltpu.VMEM((TOKENS, 128), F32),
            dma((4,)),
            dma((N_GATHER,)),
            dma((N_GATHER,)),
            dma((N_EDGE,)),
            dma((N_EDGE,)),
            dma((15,)),
            dma((15,)),
            dma((15,)),
            dma((15,)),
            dma((15,)),
            dma((15,)),
            dma((6,)),
            dma((6,)),
        ],
        compiler_params=pltpu.CompilerParams(
            collective_id=0, has_side_effects=True, vmem_limit_bytes=62 * 1024 * 1024
        ),
    )(tokens, par, w_x, w_z, w_bc, wdt)


def solution(mesh):
    torus = Mesh(mesh.devices.reshape(mesh.shape["sec"], 4, 4, 2), AXES)
    return jax.shard_map(
        per_device,
        mesh=torus,
        in_specs=(
            P(AXES, None), P(), P(FSDP, None), P(FSDP, None), P(FSDP, None), P(FSDP, None),
            P(), P(), P(), P(), P(), P(),
        ),
        out_specs=P(AXES, None),
        check_vma=False,
    )
```

time: 380 us -> 123 us (0.32)
  waiting for transfers between devices: 265 us -> 0 us
  Pallas kernels: 0 us -> 112 us
  matrix products: 35.9 us -> 0 us
  blocking collectives: 25.3 us -> 0 us
  other arithmetic: 21.2 us -> 0 us
  between operations: 13.5 us -> 0.02 us
  starting transfers between devices: 4.84 us -> 0 us
    all_gather x5 -> x0, waiting for transfers between devices: 264 us -> none  [the longest x4 161 us: entering(): pieces = jax.tree.map(lambda part: lax.all_gather(part, axis), running)]
    pallas_call x0 -> x1, Pallas kernels: none -> 112 us  [per_device(): pl.pallas_call(kernel, out_shape=jax.ShapeDtypeStruct((TOKENS, MODEL), BF...]
    dot_general x8 -> x0, matrix products: 35.9 us -> none  [the longest x4 22.5 us: per_device(): jnp.dot(normed, pieces[slot], preferred_element_type=jnp.float32)]
    all_gather x4 -> x0, blocking collectives: 25.3 us -> none  [entering(): pieces = jax.tree.map(lambda part: lax.all_gather(part, axis), running)]
    add x3 -> x0, other arithmetic: 11 us -> none  [join_carry(): earlier[1] * latter[0][:, None, None] + latter[1]]
    convert_element_type x3 -> x0, other arithmetic: 6.83 us -> none  [the longest x1 5.3 us: block_terms(): (x_conv.astype(jnp.float32) * to_end[..., None]).astype(jnp.bfloat16)]
    ppermute x2 -> x0, starting transfers between devices: 4.67 us -> none  [shifted(): lax.ppermute(value, axis, [(source, source + steps) for source in range(f...]
    mul x6 -> x0, local copies, waits for them, and re-layouts: 4.24 us -> none  [the longest x3 4.02 us: block_terms(): x_conv.astype(jnp.float32) * to_end[..., None]]
  transfers between devices with their start and end apart: 7 -> 0, of which waited for: 6 -> 0; matrix products, arithmetic and copies ran while one was open for 4% -> 0% of each run, Pallas kernels for 0% -> 0%
where the time goes in v1:
time: 123 us; the launch traced here: 122 us
  Pallas kernels  112 us (91%)
  local copies, waits for them, and re-layouts  10.2 us (8%)
    pallas_call x1, Pallas kernels, per_device(): pl.pallas_call(kernel, out_shape=jax.ShapeDtypeStruct((TOKENS, MODEL), BF...  112 us
    pad x5, local copies, waits for them, and re-layouts, line(): return jnp.pad(v, (0, width - v.shape[0]))[None]  3.41 us
    unnamed x2, local copies, waits for them, and re-layouts  3.26 us

profile of v1, /device:TPU:1, one launch (start us, length us, event | category | flops | bytes accessed | tf_op | source)
XLA Modules:
  0.0 122.4 jit_solution(9112002942622261450)
XLA Ops:
  0.0 0.7 broadcast_in_dim.18
  0.7 0.7 pad.21
  1.4 0.7 pad.23
  2.1 0.7 pad.24
  2.8 0.7 pad.25
  3.5 0.7 pad.22
  4.2 0.8 copy.13
  5.0 0.6 pad.26.wdt
  5.6 2.2 %concatenate.3.par = f32[10,2816]{1,0:T(8,128)} concatenate(f32[4,2816]{1,0:T(4,128)} %param.18, f32[1,2816]{1,0:T(1,128)S(1)} %broadcast_in_dim.18, f32[1,2816]{1,0:T(1,128)S(1)} %broadcast_in_dim.19, f32[1,2816]{1,0:T(1,128)S(1)} %broadcast_in_dim.20, f32[1,2816]{1,0:T(1,128)S(1)} %broadcast_in_dim.21, f32[1,2816]{1,0:T(1,128)S(1)} %broadcast_in_dim.22, ...), dimensions={0} | concatenate | bytes 225280 | tf_op jit(solution)/shard_map/concatenate | solution.py:491
  7.8 112.1 %shard_map.118 = bf16[256,2560]{1,0:T(8,128)(2,1)} custom-call(bf16[256,2560]{1,0:T(8,128)(2,1)} %tok.1, f32[10,2816]{1,0:T(8,128)} %concatenate.3.par, bf16[80,2560]{1,0:T(8,128)(2,1)} %wx.1, bf16[80,2560]{1,0:T(8,128)(2,1)} %wz.1, bf16[80,256]{1,0:T(8,128)(2,1)} %wbc.1, bf16[80,128]{1,0:T(8,128)(2,1)} %pad.26.wdt), custom_call_target="tpu_custom_call" | custom-call | tf_op jit(solution)/shard_map/pallas_call | solution.py:497
  119.9 2.5 %copy.15 = bf16[256,2560]{1,0:T(8,128)(2,1)} copy(bf16[256,2560]{1,0:T(8,128)(2,1)} %shard_map.118) | data formatting | bytes 2621440
  (5 shorter events, 0.1 us)

commit v2 on v1

v2 whole, which is shorter than its diff:
```python
import functools

import jax
import jax.numpy as jnp
from jax import lax
from jax.experimental import pallas as pl
from jax.experimental.pallas import tpu as pltpu
from jax.sharding import Mesh
from jax.sharding import PartitionSpec as P

AXES = ("sec", "fy", "fz", "fc")
FSDP = AXES[1:]
MESH = pl.DeviceIdType.MESH
F32, BF16 = jnp.float32, jnp.bfloat16

MODEL = 2560
HALF = 1280
STATE = 128
HEADDIM = 64
HALF_HEADS = 20
TOKENS = 256
CHIP_TOKENS = 512
HALO = 16
CHUNK = 128
CHUNKS = 4
SHARD = 80
FIRST = HALF + 2 * STATE
EPS = 1e-05
LOG2E = 1.4426950408889634
SPLIT = 48
DIRECT = 96
TILE = 16
WIDTHS = (1024, 512, 768, 512)
NARROW = 2 * STATE
SPOTS = (
    (-1, 0), (1, 0), (0, -1), (0, 1), (2, 0), (-1, -1), (-1, 1), (1, -1), (1, 1), (0, 2), (2, -1), (2, 1), (-1, 2), (1, 2), (2, 2)
)
PER_GATHER = 18 + 15 + 45
N_GATHER = PER_GATHER * len(WIDTHS)
N_EDGE = 20


def dot(a, b, **kw):
    return jnp.dot(a, b, preferred_element_type=F32, **kw)


def contract(a, b, da, db):
    return lax.dot_general(a, b, (((da,), (db,)), ((), ())), preferred_element_type=F32)


def aligned(i, n):
    return pl.multiple_of(i, n)


class Gather:
    def __init__(self, w, sends, recvs, base, where):
        self.w, self.sends, self.recvs, self.next = w, sends, recvs, base
        self.x, self.y, self.z, self.c = where
        self.all = []
        self.m = {}
        for kind in ("d", "q"):
            for sign in (1, -1):
                self.ring(kind + "p1", sign, 0, 0, 0)
                for o in (0, -1, 1, 2):
                    self.ring(kind + "p2", sign, 1, o, 0)
        self.ring("df1", 1, 0, -1, 0, 0, SPLIT)
        self.ring("df1", -1, 0, 1, 0, SPLIT, DIRECT)
        self.ring("df2", 1, 1, 0, -1)
        self.ring("df2", -1, 1, 1, 1)
        for o in (-1, 2):
            self.ring("df2", 1, 1, o, -1, 0, SPLIT)
            self.ring("df2", -1, 1, o, 1, SPLIT, DIRECT)
        self.ring("qf1", 1, 0, -1, 0)
        for sign, o in ((1, 0), (1, 2), (-1, -1), (-1, 1)):
            self.ring("qf2", sign, 1, o, -sign)
        for i, spot in enumerate(SPOTS):
            for sign in (1, -1):
                self.cross("xp", sign, i, spot, 0)
            sign = 1 if i % 2 == 0 else -1
            self.cross("xf", sign, i, spot, 1)

    def place(self, o1, o2):
        c = self.c
        yy = (self.y + (o1 * (1 - c) + o2 * c + 4)) % 4
        zz = (self.z + (o2 * (1 - c) + o1 * c + 4)) % 4
        return yy * 4 + zz

    def tile(self, q):
        return pl.ds(aligned(DIRECT + TILE * ((self.x + (q + 4)) % 4), TILE), TILE)

    def make(self, src, land, dev, key):
        k = self.next
        self.next += 1
        out = pltpu.make_async_remote_copy(src, src, self.sends.at[k], self.recvs.at[k], device_id=dev, device_id_type=MESH)
        back = pltpu.make_async_remote_copy(land, land, self.sends.at[k], self.recvs.at[k], device_id=dev, device_id_type=MESH)
        self.m[key] = (out, back)
        self.all.append(out)

    def ring(self, kind, sign, which, o1, o2, lo=0, hi=DIRECT):
        c = self.c
        along_y = 1 - c if which == 0 else c
        dev = (self.x, (self.y + (sign * along_y + 4)) % 4, (self.z + (sign * (1 - along_y) + 4)) % 4, c)
        rows = pl.ds(lo, hi - lo) if kind[0] == "d" else self.tile(0)
        r1, r2 = (o1 - sign, o2) if which == 0 else (o1, o2 - sign)
        self.make(self.w.at[self.place(o1, o2), rows, :], self.w.at[self.place(r1, r2), rows, :], dev, (kind, sign, o1))

    def cross(self, kind, sign, i, spot, away):
        dev = ((self.x + (sign + 4)) % 4, self.y, self.z, self.c)
        at = self.place(*spot)
        src, land = self.w.at[at, self.tile(-sign * away), :], self.w.at[at, self.tile(-sign * (away + 1)), :]
        self.make(src, land, dev, (kind, sign, i))

    def go(self, kind, sign, o):
        self.m[kind, sign, o][0].start()

    def got(self, kind, sign, o):
        self.m[kind, sign, o][1].wait_recv()

    def both(self, kind, o):
        self.go(kind, 1, o)
        self.go(kind, -1, o)

    def spread(self, *spots):
        for spot in spots:
            self.both("xp", SPOTS.index(spot))

    def qb(self):
        self.both("qp1", 0)
        self.both("qp2", 0)

    def q0(self):
        self.got("qp1", 1, 0)
        self.go("qf1", 1, -1)
        self.both("qp2", -1)
        self.spread((-1, 0))

    def q1(self):
        self.got("qp1", -1, 0)
        self.both("qp2", 1)
        self.spread((1, 0))

    def q2(self):
        self.got("qp2", 1, 0)
        self.go("qf2", 1, 0)
        self.spread((0, -1))
        self.got("qp2", -1, 0)
        self.spread((0, 1))

    def q3(self):
        self.got("qf1", 1, -1)
        self.both("qp2", 2)
        self.spread((2, 0))

    def q4(self):
        self.got("qp2", 1, -1)
        self.spread((-1, -1))
        self.got("qp2", -1, -1)
        self.go("qf2", -1, -1)
        self.spread((-1, 1))
        self.got("qp2", 1, 1)
        self.spread((1, -1))
        self.got("qp2", -1, 1)
        self.go("qf2", -1, 1)
        self.spread((1, 1))

    def q5(self):
        self.got("qf2", 1, 0)
        self.spread((0, 2))
        self.got("qp2", 1, 2)
        self.go("qf2", 1, 2)
        self.spread((2, -1))
        self.got("qp2", -1, 2)
        self.spread((2, 1))

    def q6(self):
        self.got("qf2", -1, -1)
        self.spread((-1, 2))
        self.got("qf2", -1, 1)
        self.spread((1, 2))
        self.got("qf2", 1, 2)
        self.spread((2, 2))

    def x_some(self, lo, hi):
        for i in range(lo, hi):
            for sign in (1, -1):
                self.got("xp", sign, i)
            self.go("xf", 1 if i % 2 == 0 else -1, i)

    def xa(self):
        self.x_some(0, 5)

    def xb(self):
        self.x_some(5, 10)

    def xc(self):
        self.x_some(10, 15)

    def xd(self):
        for i in range(15):
            self.got("xf", 1 if i % 2 == 0 else -1, i)

    def db(self):
        self.both("dp1", 0)

    def dc(self):
        self.both("dp2", 0)

    def d0(self):
        self.got("dp1", 1, 0)
        self.go("df1", 1, -1)
        self.both("dp2", -1)

    def d1(self):
        self.got("dp1", -1, 0)
        self.go("df1", -1, 1)
        self.both("dp2", 1)

    def d2(self):
        self.got("dp2", 1, 0)
        self.go("df2", 1, 0)
        self.got("dp2", -1, 0)

    def d3(self):
        self.got("df1", 1, -1)
        self.got("df1", -1, 1)
        self.both("dp2", 2)

    def d4(self):
        self.got("dp2", 1, -1)
        self.go("df2", 1, -1)
        self.got("dp2", -1, -1)
        self.go("df2", -1, -1)

    def d5(self):
        self.got("dp2", 1, 1)
        self.got("dp2", -1, 1)
        self.go("df2", -1, 1)

    def d6(self):
        self.got("dp2", 1, 2)
        self.go("df2", 1, 2)
        self.got("dp2", -1, 2)
        self.go("df2", -1, 2)

    def d7(self):
        for sign, o in ((1, 0), (-1, 1), (1, -1), (-1, -1), (1, 2), (-1, 2)):
            self.got("df2", sign, o)

    def drain(self):
        for out in self.all:
            out.wait_send()


def silu(v):
    return v / (1.0 + jnp.exp(-v))


def interleave(services, work):
    done = 0
    for i, service in enumerate(services):
        service()
        while done < len(work) and done * len(services) < (i + 1) * len(work):
            work[done]()
            done += 1
    for item in work[done:]:
        item()


def steady(now, then):
    early = [now.q5, now.d0, now.d1, now.xa, now.q6, now.d2, now.d3]
    if then is None:
        return early + [now.xb, now.d4, now.d5, now.d6, now.xc, now.d7, now.xd]
    middle = [then.qb, now.xb, now.d4, now.d5, then.q0, then.q1, then.q2, now.d6, then.db, then.dc]
    return early + middle + [now.xc, then.q3, then.q4, now.d7, now.xd]


def kernel(
    tok_hbm, cw, cb, pg, ng, dtb, alog, dskip, wx, wz, wbc, wdt_t, out,
    w0, w1, w2, w3, tok, wdt, square, small, nt, pre, xc, bc, y, zs, stl, sbuf, rbuf, pbuf, st0, st0f,
    dts, cum, row, e2, tmp, dec, dsk, cs, cr, drow, pfx, xt, xtr, xcs, xcr,
    gs, gr, ss, sss, ssr,
    local_sem, gsend, grecv, esend, erecv, asend, arecv, csend, crecv, bsend, brecv, xsend, xrecv,
):
    x, yy, zz, c = [lax.axis_index(a) for a in AXES]
    plane = yy * 4 + zz
    chip = x * 16 + plane
    sib = (x, yy, zz, 1 - c)

    def chip_dev(s):
        return (s // 16, (s // 4) % 4, s % 4, c)

    def plane_dev(q):
        return (x, q // 4, q % 4, c)

    after, before = (chip + 1) % 64, (chip + 63) % 64

    def remote(src, dst, send, recv, dev):
        return pltpu.make_async_remote_copy(src, dst, send, recv, device_id=dev, device_id_type=MESH)

    barrier = pltpu.get_barrier_semaphore()
    targets = [sib, chip_dev(after), chip_dev(before)]
    targets += [plane_dev((plane + o) % 16) for o in range(1, 16)]
    targets += [((x + o) % 4, yy, zz, c) for o in range(1, 4)]
    for dev in targets:
        pl.semaphore_signal(barrier, inc=1, device_id=dev, device_id_type=MESH)

    def half(core, at, n):
        return pl.ds(aligned(core * HALF + at, 128), n)

    def state_half(core):
        return pl.ds(aligned(core * STATE, 128), STATE)

    def pieces(core):
        return (
            (wbc.at[:, state_half(core)], w0, 0, STATE),
            (wx.at[:, half(core, 0, 768)], w0, NARROW, 768),
            (wx.at[:, half(core, 768, 512)], w1, 0, 512),
            (wz.at[:, half(core, 0, 768)], w2, 0, 768),
            (wz.at[:, half(core, 768, 512)], w3, 0, 512),
            (wdt, w0, STATE, STATE),
        )

    mine = pl.ds(aligned(c * SHARD, 16), SHARD)
    locals_ = [
        pltpu.make_async_copy(src, w.at[plane, mine, pl.ds(at, n)], local_sem.at[k])
        for k, (src, w, at, n) in enumerate(pieces(c))
    ]
    gives = [
        remote(src, w.at[plane, mine, pl.ds(at, n)], esend.at[k], erecv.at[k], sib)
        for k, (src, w, at, n) in enumerate(pieces(1 - c))
    ]
    load = pltpu.make_async_copy(tok_hbm, tok, local_sem.at[6])
    for copy in locals_[:3]:
        copy.start()
    load.start()
    for copy in locals_[3:5]:
        copy.start()
    square[...] = jnp.zeros((STATE, STATE), F32)
    square[0:40, 0:SHARD] = wdt_t[...].astype(F32)
    wdt[...] = square[...].T[0:SHARD, :].astype(BF16)
    locals_[5].start()
    small[...] = jnp.zeros((8, STATE), F32)
    for k, ref in enumerate((dtb, alog, dskip)):
        small[k : k + 1, 0:40] = ref[...]

    pl.semaphore_wait(barrier, len(targets))
    order = (0, 5, 1, 2, 3, 4)
    for k in order:
        gives[k].start()

    def ready(ks):
        for k in ks:
            locals_[k].wait()
            gives[k].wait_recv()

    where = (x, yy, zz, c)
    g = [Gather(w, gsend, grecv, k * PER_GATHER, where) for k, w in enumerate((w0, w1, w2, w3))]
    ready((0, 5, 1))
    g[0].qb()
    g[0].db()
    base_rows = aligned(HALO + c * TOKENS, 16)
    gain = pg[...]

    def normalize(r, carry):
        v = tok[pl.ds(aligned(r * 32, 32), 32), :].astype(F32)
        mean = jnp.mean(v * v, axis=-1, keepdims=True)
        nt[pl.ds(aligned(base_rows + r * 32, 16), 32), :] = (v * lax.rsqrt(mean + EPS) * gain).astype(BF16)
        return carry

    load.wait()
    lax.fori_loop(0, TOKENS // 32, normalize, 0)
    tok_rows = nt.at[pl.ds(base_rows, TOKENS), :]
    swap = remote(tok_rows, tok_rows, esend.at[6], erecv.at[6], sib)
    swap.start()
    g[0].q0()
    g[0].q1()
    g[0].dc()
    g[0].q2()

    kk = lax.broadcasted_iota(jnp.int32, (2 * STATE, 256), 0) % STATE
    for j in range(HALF // 256):
        ll = (lax.broadcasted_iota(jnp.int32, (2 * STATE, 256), 1) + j * 256) // HEADDIM
        e2[:, j * 256 : (j + 1) * 256] = jnp.where(kk == ll, 1.0, 0.0).astype(BF16)

    def halves(v):
        hi = v.astype(BF16)
        lo = (v - hi.astype(F32)).astype(BF16)
        return jnp.concatenate([hi, lo], axis=1)

    g[0].d0()
    g[0].d1()
    swap.wait_recv()
    halo_src, halo_dst = nt.at[pl.ds(CHIP_TOKENS, HALO), :], nt.at[pl.ds(0, HALO), :]
    halo = remote(halo_src, halo_dst, esend.at[7], erecv.at[7], chip_dev(after))
    halo.start()
    for service in (g[0].q3, g[0].q4, g[0].xa, g[0].q5, g[0].d2, g[0].d3, g[0].q6):
        service()
    ready((2,))
    g[1].qb()
    roll_by = (STATE - HALF_HEADS * c) % STATE
    skip = pltpu.roll(jnp.broadcast_to(small[2:3, :], (8, STATE)), roll_by, 1)
    dsk[...] = dot(halves(skip), e2[...])
    for service in (g[0].xb, g[0].d4, g[0].d5, g[1].q0, g[1].q1, g[1].q2, g[0].d6, g[1].db, g[1].dc, g[0].xc):
        service()
    halo.wait_recv()

    @pl.when(chip == 0)
    def _():
        nt[0:HALO, :] = jnp.zeros((HALO, MODEL), BF16)

    for service in (g[1].q3, g[1].q4, g[0].d7, g[0].xd):
        service()

    def project(w, at):
        def body(j, carry):
            lanes = pl.ds(aligned(j * 256, 256), 256)
            pre[:, pl.ds(aligned(at + j * 256, 256), 256)] = dot(nt[...], w[:, :, lanes].reshape(MODEL, 256))
            return carry

        return body

    def loop(lo, hi, body):
        return lambda: lax.fori_loop(lo, hi, body, 0)

    tri = jnp.where(
        lax.broadcasted_iota(jnp.int32, (CHUNK, CHUNK), 0) >= lax.broadcasted_iota(jnp.int32, (CHUNK, CHUNK), 1), 1.0, 0.0
    )

    def steps(i, carry):
        rate = jnp.exp(small[1:2, :]) * LOG2E
        rows = pl.ds(aligned(i * CHUNK, CHUNK), CHUNK)
        raw = pre[pl.ds(aligned(HALO + i * CHUNK, 16), CHUNK), STATE:NARROW] + small[0:1, :]
        dt = jnp.maximum(raw, 0.0) + jnp.log1p(jnp.exp(-jnp.abs(raw)))
        total = dot(tri, pltpu.roll(dt * rate, roll_by, 1), precision=lax.Precision.HIGHEST)
        dt = pltpu.roll(dt, roll_by, 1)
        dts[rows, :] = dt
        cum[rows, :] = total
        row[i] = (total + jnp.log(dt) * LOG2E).T
        return carry

    totals, totals_in = [], []
    for o in range(1, 16):
        q, p = (plane + o) % 16, (plane + (16 - o)) % 16
        totals.append(remote(cs, cr.at[plane], csend.at[o - 1], crecv.at[o - 1], plane_dev(q)))
        totals_in.append(remote(cs, cr.at[p], csend.at[o - 1], crecv.at[o - 1], plane_dev(q)))

    def send_totals():
        running = jnp.zeros((1, STATE), F32)
        for i in range(CHUNKS):
            last = cum[i * CHUNK + CHUNK - 1 : (i + 1) * CHUNK, :]
            tmp[i : i + 1, :] = last
            tmp[4 + i : 5 + i, :] = running
            running = running + last
        cs[...] = jnp.broadcast_to(running, (8, STATE))
        cr[plane] = jnp.broadcast_to(running, (8, STATE))
        for copy in totals:
            copy.start()
        dec[...] = dot(halves(jnp.exp2(-tmp[...])), e2[...])

    def convolve(at, col):
        taps = [cw[k : k + 1, col] for k in range(4)]
        offset = cb[0:1, col]
        parts = []
        for r in range(0, CHIP_TOKENS, CHUNK):
            v = offset
            for k in range(4):
                v = v + taps[k] * pre[HALO - 3 + k + r : HALO - 3 + k + r + CHUNK, at]
            parts.append(silu(v).astype(BF16))
        return parts

    swap_bc = remote(bc.at[c], bc.at[c], esend.at[8], erecv.at[8], sib)

    def conv_bc():
        for r, part in enumerate(convolve(pl.ds(0, STATE), pl.ds(aligned(2 * HALF + c * STATE, 128), STATE))):
            bc[c, r * CHUNK : (r + 1) * CHUNK, :] = part
        swap_bc.start()

    def conv_x(j, carry):
        parts = convolve(pl.ds(aligned(NARROW + j * 128, 128), 128), pl.ds(aligned(c * HALF + j * 128, 128), 128))
        for r, part in enumerate(parts):
            xc[r * CHUNK : (r + 1) * CHUNK, pl.ds(aligned(j * 128, 128), 128)] = part
        return carry

    def states(lo, hi):
        def body(i, carry):
            rows = pl.ds(aligned(i * CHUNK, CHUNK), CHUNK)
            to_end = halves(jnp.exp2(cum[rows, :] - tmp[pl.ds(i, 1), :]) * dts[rows, :])
            b = bc[0, rows, :]
            for j in range(lo, hi):
                at = slice(j * 256, (j + 1) * 256)
                weighted = (dot(to_end, e2[:, at]) * xc[rows, at].astype(F32)).astype(BF16)
                stl[i + 1, :, at] = stl[i, :, at] * dec[pl.ds(i, 1), at] + contract(b, weighted, 0, 0)
            return carry

        return body

    parts_out, parts_in = [], []
    for o in range(1, 16):
        q, p = (plane + o) % 16, (plane + (16 - o)) % 16
        parts_out.append(remote(sbuf.at[q], rbuf.at[plane], asend.at[o - 1], arecv.at[o - 1], plane_dev(q)))
        parts_in.append(remote(sbuf.at[q], rbuf.at[p], asend.at[o - 1], arecv.at[o - 1], plane_dev(q)))

    def send_parts():
        for q in range(16):
            sbuf[q] = stl[CHUNKS, q * 8 : (q + 1) * 8, :].astype(BF16)
        rbuf[plane] = sbuf[plane]
        for copy in parts_out:
            copy.start()

    causal = lax.broadcasted_iota(jnp.int32, (CHUNK, CHUNK), 0) >= lax.broadcasted_iota(jnp.int32, (CHUNK, CHUNK), 1)
    low = jnp.where(lax.broadcasted_iota(jnp.int32, (CHUNK, 128), 1) < HEADDIM, 1.0, 0.0).astype(BF16)
    high = (1.0 - low.astype(F32)).astype(BF16)

    def intra(lo, hi):
        def body(i, carry):
            rows = pl.ds(aligned(i * CHUNK, CHUNK), CHUNK)
            inner = contract(bc[1, rows, :], bc[0, rows, :], 1, 1)
            for pair in range(lo, hi):
                both = []
                for h in (2 * pair, 2 * pair + 1):
                    gap = row[i, h : h + 1, :] - cum[rows, h : h + 1]
                    both.append((jnp.exp2(jnp.where(causal, gap, -1e30)) * inner).astype(BF16))
                at = slice(pair * 128, (pair + 1) * 128)
                xp = xc[rows, at]
                spread = jnp.concatenate([xp * low, xp * high], axis=0)
                y[rows, at] = dot(jnp.concatenate(both, axis=1), spread) + dsk[0:1, at] * xp.astype(F32)
            return carry

        return body

    def zero_states():
        stl[0] = jnp.zeros((STATE, HALF), F32)

    work = [
        loop(0, 1, project(w0, 0)), loop(0, CHUNKS, steps), send_totals, conv_bc,
        loop(1, 2, project(w0, 0)), loop(2, 4, project(w0, 0)), zero_states, loop(0, 6, conv_x), swap_bc.wait_recv,
        loop(0, CHUNKS, states(0, 3)), loop(0, 2, intra(0, 6)), loop(2, CHUNKS, intra(0, 6)),
    ]
    ready((3, 4))
    interleave(steady(g[1], g[2]), work)

    work = [
        loop(0, 2, project(w1, 1024)), loop(6, 10, conv_x), loop(0, CHUNKS, states(3, 5)), send_parts,
        loop(0, 2, intra(6, 10)), loop(2, CHUNKS, intra(6, 10)),
    ]
    flow = steady(g[2], g[3])
    for item in work[:4]:
        item()
        flow.pop(0)()
    interleave(flow, work[4:])

    for copy in totals_in:
        copy.wait_recv()
    for copy in parts_in:
        copy.wait_recv()
    drow[...] = dot(halves(jnp.exp2(-cr[:, 0, :])), e2[...])

    def prefix(k, state):
        pfx[k] = state
        return state * drow[pl.ds(k, 1), :] + rbuf[k].astype(F32)

    whole = lax.fori_loop(0, 16, prefix, jnp.zeros((8, HALF), F32))
    xt[...] = whole
    plane_total = jnp.zeros((8, STATE), F32)
    for k in range(16):
        plane_total = plane_total + cr[k]
    xcs[...] = plane_total
    sec_out, sec_in = [], []
    for o in range(1, 4):
        q, p = (x + o) % 4, (x + (4 - o)) % 4
        for k, (src, dst) in enumerate(((xt, xtr), (xcs, xcr))):
            n = 2 * (o - 1) + k
            sec_out.append(remote(src, dst.at[x], xsend.at[n], xrecv.at[n], (q, yy, zz, c)))
            sec_in.append(remote(src, dst.at[p], xsend.at[n], xrecv.at[n], (q, yy, zz, c)))
    for copy in sec_out:
        copy.start()
    xtr[x] = whole
    xcr[x] = plane_total

    def zdot(w, at):
        def body(j, carry):
            lanes = pl.ds(aligned(j * 256, 256), 256)
            v = dot(nt[HALO:, :], w[:, :, lanes].reshape(MODEL, 256))
            zs[:, pl.ds(aligned(at + j * 256, 256), 256)] = v
            return carry

        return body

    flow = steady(g[3], None)
    interleave(flow[:6], [loop(0, 2, zdot(w2, 0))])
    for copy in sec_in:
        copy.wait_recv()
    enter = jnp.zeros((8, HALF), F32)
    for k in range(3):
        moved = enter * dot(halves(jnp.exp2(-xcr[k])), e2[...]) + xtr[k]
        enter = jnp.where(k < x, moved, enter)

    def begin_states(k, state):
        pbuf[k] = (pfx[k] + state).astype(BF16)
        return state * drow[pl.ds(k, 1), :]

    lax.fori_loop(0, 16, begin_states, enter)
    st0[plane] = pbuf[plane]
    starts_out, starts_in = [], []
    for o in range(1, 16):
        q, p = (plane + o) % 16, (plane + (16 - o)) % 16
        starts_out.append(remote(pbuf.at[q], st0.at[plane], bsend.at[o - 1], brecv.at[o - 1], plane_dev(q)))
        starts_in.append(remote(pbuf.at[q], st0.at[p], bsend.at[o - 1], brecv.at[o - 1], plane_dev(q)))
    for copy in starts_out:
        copy.start()
    interleave(flow[6:], [loop(2, 3, zdot(w2, 0))])
    lax.fori_loop(0, 2, zdot(w3, 768), 0)
    for copy in starts_in:
        copy.wait_recv()
    for k in range(16):
        st0f[k * 8 : (k + 1) * 8, :] = st0[k].astype(F32)

    def finish(i, r, theirs):
        rows = pl.ds(aligned(i * CHUNK, CHUNK), CHUNK)
        reach = halves(jnp.exp2(-cum[rows, :]))
        cc = bc[1, rows, :]
        total = jnp.zeros((CHUNK, 128), F32)
        for j in range(HALF // 256):
            at = slice(j * 256, (j + 1) * 256)
            state = (stl[i, :, at] + st0f[:, at] * dec[pl.ds(CHUNKS + i, 1), at]).astype(BF16)
            gated = (y[rows, at] + dot(cc, state) * dot(reach, e2[:, at])) * silu(zs[rows, at])
            if theirs:
                gs[r * CHUNK : (r + 1) * CHUNK, at] = gated.astype(BF16)
            else:
                y[rows, at] = gated
            squares = gated * gated
            total = total + squares[:, 0:128] + squares[:, 128:256]
        if theirs:
            sss[r * CHUNK : (r + 1) * CHUNK, :] = total
        else:
            ss[r * CHUNK : (r + 1) * CHUNK, :] = total

    swaps = []
    for r in range(2):
        finish((1 - c) * 2 + r, r, True)
        for k, (a, b) in enumerate(((gs, gr), (sss, ssr))):
            part = pl.ds(r * CHUNK, CHUNK)
            n = 10 + 2 * r + k
            swaps.append(remote(a.at[part, :], b.at[part, :], esend.at[n], erecv.at[n], sib))
            swaps[-1].start()
    for r in range(2):
        finish(c * 2 + r, r, False)
    for copy in swaps:
        copy.wait_recv()
    mean = jnp.sum(ss[...] + ssr[...], axis=-1, keepdims=True) * (1.0 / MODEL)
    scale = lax.rsqrt(mean + EPS)
    ours = pl.ds(aligned(c * TOKENS, TOKENS), TOKENS)
    for j in range(HALF // 256):
        at = slice(j * 256, (j + 1) * 256)
        spot = half(c, j * 256, 256)
        out[:, spot] = (y[ours, at] * scale * ng[0:1, spot]).astype(BF16)
        spot = half(1 - c, j * 256, 256)
        out[:, spot] = (gr[:, at].astype(F32) * scale * ng[0:1, spot]).astype(BF16)

    for gather in g:
        gather.drain()
    for copy in gives + [swap, halo, swap_bc] + totals + parts_out + sec_out + starts_out + swaps:
        copy.wait_send()


def per_device(
    tokens, pre_gain, w_z, w_x, w_bc, w_dt, conv_weight, conv_bias, dt_bias, a_log, d_skip, norm_gain
):
    lines = [v.reshape(1, -1) for v in (conv_bias, pre_gain, norm_gain, dt_bias, a_log, d_skip)]
    vmem, anywhere = pl.BlockSpec(memory_space=pltpu.VMEM), pl.BlockSpec(memory_space=pl.ANY)
    dma = pltpu.SemaphoreType.DMA
    return pl.pallas_call(
        kernel,
        out_shape=jax.ShapeDtypeStruct((TOKENS, MODEL), BF16),
        in_specs=[anywhere] + [vmem] * 7 + [anywhere] * 3 + [vmem],
        out_specs=vmem,
        scratch_shapes=[pltpu.VMEM((16, 2 * SHARD, n), BF16) for n in WIDTHS]
        + [
            pltpu.VMEM((TOKENS, MODEL), BF16),
            pltpu.VMEM((SHARD, STATE), BF16),
            pltpu.VMEM((STATE, STATE), F32),
            pltpu.VMEM((8, STATE), F32),
            pltpu.VMEM((HALO + CHIP_TOKENS, MODEL), BF16),
            pltpu.VMEM((HALO + CHIP_TOKENS, FIRST), F32),
            pltpu.VMEM((CHIP_TOKENS, HALF), BF16),
            pltpu.VMEM((2, CHIP_TOKENS, STATE), BF16),
            pltpu.VMEM((CHIP_TOKENS, HALF), F32),
            pltpu.VMEM((CHIP_TOKENS, HALF), F32),
            pltpu.VMEM((CHUNKS + 1, STATE, HALF), F32),
            pltpu.VMEM((16, 8, HALF), BF16),
            pltpu.VMEM((16, 8, HALF), BF16),
            pltpu.VMEM((16, 8, HALF), BF16),
            pltpu.VMEM((16, 8, HALF), BF16),
            pltpu.VMEM((STATE, HALF), F32),
            pltpu.VMEM((CHIP_TOKENS, STATE), F32),
            pltpu.VMEM((CHIP_TOKENS, STATE), F32),
            pltpu.VMEM((CHUNKS, STATE, CHUNK), F32),
            pltpu.VMEM((2 * STATE, HALF), BF16),
            pltpu.VMEM((8, STATE), F32),
            pltpu.VMEM((8, HALF), F32),
            pltpu.VMEM((8, HALF), F32),
            pltpu.VMEM((8, STATE), F32),
            pltpu.VMEM((16, 8, STATE), F32),
            pltpu.VMEM((16, HALF), F32),
            pltpu.VMEM((16, 8, HALF), F32),
            pltpu.VMEM((8, HALF), F32),
            pltpu.VMEM((4, 8, HALF), F32),
            pltpu.VMEM((8, STATE), F32),
            pltpu.VMEM((4, 8, STATE), F32),
            pltpu.VMEM((TOKENS, HALF), BF16),
            pltpu.VMEM((TOKENS, HALF), BF16),
            pltpu.VMEM((TOKENS, 128), F32),
            pltpu.VMEM((TOKENS, 128), F32),
            pltpu.VMEM((TOKENS, 128), F32),
            dma((7,)),
            dma((N_GATHER,)),
            dma((N_GATHER,)),
            dma((N_EDGE,)),
            dma((N_EDGE,)),
            dma((15,)),
            dma((15,)),
            dma((15,)),
            dma((15,)),
            dma((15,)),
            dma((15,)),
            dma((6,)),
            dma((6,)),
        ],
        compiler_params=pltpu.CompilerParams(
            collective_id=0, has_side_effects=True, vmem_limit_bytes=62 * 1024 * 1024
        ),
    )(tokens, conv_weight, *lines, w_x, w_z, w_bc, w_dt.T)


def solution(mesh):
    torus = Mesh(mesh.devices.reshape(mesh.shape["sec"], 4, 4, 2), AXES)
    return jax.shard_map(
        per_device,
        mesh=torus,
        in_specs=(
            P(AXES, None), P(), P(FSDP, None), P(FSDP, None), P(FSDP, None), P(FSDP, None),
            P(), P(), P(), P(), P(), P(),
        ),
        out_specs=P(AXES, None),
        check_vma=False,
    )
```

time: 123 us -> 116 us (0.943)
  local copies, waits for them, and re-layouts: 10.2 us -> 6.39 us
  Pallas kernels: 112 us -> 109 us
    pad x6 -> x0, local copies, waits for them, and re-layouts: 4.02 us -> none  [the longest x5 3.41 us: line(): return jnp.pad(v, (0, width - v.shape[0]))[None]]
    reshape x0 -> x3, local copies, waits for them, and re-layouts: none -> 3.93 us  [per_device(): v.reshape(1, -1)]
    pallas_call x1, Pallas kernels: 112 us -> 109 us  [per_device(): pl.pallas_call(kernel, out_shape=jax.ShapeDtypeStruct((TOKENS, MODEL), BF...]
    concatenate x1 -> x0, local copies, waits for them, and re-layouts: 2.17 us -> none  [per_device(): jnp.concatenate([conv_weight, line(conv_bias), line(pre_gain), line(norm_...]
    unnamed x2 -> x1, local copies, waits for them, and re-layouts: 3.26 us -> 2.46 us
where the time goes in v2:
time: 116 us
  Pallas kernels  109 us (94%)
  local copies, waits for them, and re-layouts  6.39 us (6%)
    pallas_call x1, Pallas kernels, per_device(): pl.pallas_call(kernel, out_shape=jax.ShapeDtypeStruct((TOKENS, MODEL), BF...  109 us
    reshape x3, local copies, waits for them, and re-layouts, per_device(): v.reshape(1, -1)  3.93 us
    unnamed x1, local copies, waits for them, and re-layouts  2.46 us

profile of v2, /device:TPU:1, one launch (start us, length us, event | category | flops | bytes accessed | tf_op | source)
XLA Modules:
  0.0 115.6 jit_solution(17432339655100309453)
XLA Ops:
  0.0 1.3 %reshape.19.pg = f32[1,2560]{1,0:T(1,128)} reshape(f32[2560]{0:T(1024)} %param.13) | data formatting | bytes 20480 | tf_op jit(solution)/shard_map/reshape | solution.py:669
  1.3 1.3 %reshape.20.ng = f32[1,2560]{1,0:T(1,128)} reshape(f32[2560]{0:T(1024)} %param.23) | data formatting | bytes 20480 | tf_op jit(solution)/shard_map/reshape | solution.py:669
  2.6 1.3 %reshape.18.cb = f32[1,2816]{1,0:T(1,128)} reshape(f32[2816]{0:T(1024)} %param.19) | data formatting | bytes 22528 | tf_op jit(solution)/shard_map/reshape | solution.py:669
  3.9 109.2 %shard_map.118 = bf16[256,2560]{1,0:T(8,128)(2,1)} custom-call(bf16[256,2560]{1,0:T(8,128)(2,1)} %tok_hbm.1, f32[4,2816]{1,0:T(4,128)} %cw.1, f32[1,2816]{1,0:T(1,128)} %reshape.18.cb, f32[1,2560]{1,0:T(1,128)} %reshape.19.pg, f32[1,2560]{1,0:T(1,128)} %reshape.20.ng, f32[1,40]{1,0:T(1,128)} %bitcast.5, f32[1,40]{1,0:T(1,128)} %bitcast.6, f32[1,40]{1,0:T(1,128)} %bitcast.7, ...), custom_call_target="tpu_custom_call" | custom-call | tf_op jit(solution)/shard_map/pallas_call | solution.py:672
  113.2 2.5 %copy.14 = bf16[256,2560]{1,0:T(8,128)(2,1)} copy(bf16[256,2560]{1,0:T(8,128)(2,1)} %shard_map.118) | data formatting | bytes 2621440

commit v3 on v2

--- a/solution.py
+++ b/solution.py
@@ -27,17 +27,18 @@
 FIRST = HALF + 2 * STATE
 EPS = 1e-05
 LOG2E = 1.4426950408889634
-SPLIT = 48
-DIRECT = 96
-TILE = 16
 WIDTHS = (1024, 512, 768, 512)
+TILES = (16, 16, 16, 32)
 NARROW = 2 * STATE
 SPOTS = (
     (-1, 0), (1, 0), (0, -1), (0, 1), (2, 0), (-1, -1), (-1, 1), (1, -1), (1, 1), (0, 2), (2, -1), (2, 1), (-1, 2), (1, 2), (2, 2)
 )
-PER_GATHER = 18 + 15 + 45
-N_GATHER = PER_GATHER * len(WIDTHS)
-N_EDGE = 20
+GROUPS = {
+    "d0": 1, "d1": 1, "d2": 2, "d3": 1, "d4": 2, "d5": 2, "d6": 2, "d7": 4,
+    "q0": 1, "q1": 1, "q2": 2, "q3": 1, "q4": 4, "q5": 3, "q6": 3, "xa": 10, "xb": 10, "xc": 10, "xd": 15
+}
+NAMES = list(GROUPS)
+N_EDGE = 14
 
 
 def dot(a, b, **kw):
@@ -53,31 +54,35 @@
 
 
 class Gather:
-    def __init__(self, w, sends, recvs, base, where):
-        self.w, self.sends, self.recvs, self.next = w, sends, recvs, base
+    def __init__(self, w, sends, recvs, number, where):
+        self.w, self.sent, self.recvs, self.number = w, sends.at[number], recvs, number
         self.x, self.y, self.z, self.c = where
-        self.all = []
+        self.eager = number == 0
+        self.rows = TILES[number]
+        direct = self.direct = 2 * SHARD - 4 * self.rows
+        split = direct // 2
         self.m = {}
         for kind in ("d", "q"):
             for sign in (1, -1):
-                self.ring(kind + "p1", sign, 0, 0, 0)
-                for o in (0, -1, 1, 2):
-                    self.ring(kind + "p2", sign, 1, o, 0)
-        self.ring("df1", 1, 0, -1, 0, 0, SPLIT)
-        self.ring("df1", -1, 0, 1, 0, SPLIT, DIRECT)
-        self.ring("df2", 1, 1, 0, -1)
-        self.ring("df2", -1, 1, 1, 1)
+                self.ring(kind + "p1", sign, 0, 0, 0, "0" if sign == 1 else "1")
+                for o, group in zip((0, -1, 1, 2), "2456" if kind == "d" else "2445"):
+                    self.ring(kind + "p2", sign, 1, o, 0, group)
+        self.ring("df1", 1, 0, -1, 0, "3", 0, split)
+        self.ring("df1", -1, 0, 1, 0, "3", split, direct)
+        self.ring("df2", 1, 1, 0, -1, "7")
+        self.ring("df2", -1, 1, 1, 1, "7")
         for o in (-1, 2):
-            self.ring("df2", 1, 1, o, -1, 0, SPLIT)
-            self.ring("df2", -1, 1, o, 1, SPLIT, DIRECT)
-        self.ring("qf1", 1, 0, -1, 0)
-        for sign, o in ((1, 0), (1, 2), (-1, -1), (-1, 1)):
-            self.ring("qf2", sign, 1, o, -sign)
+            self.ring("df2", 1, 1, o, -1, "7", 0, split)
+            self.ring("df2", -1, 1, o, 1, "7", split, direct)
+        self.turn = 1 if number % 2 == 0 else -1
+        self.ring("qf1", self.turn, 0, -self.turn, 0, "3")
+        for sign, o, group in ((1, 0, "5"), (1, 2, "6"), (-1, -1, "6"), (-1, 1, "6")):
+            self.ring("qf2", sign, 1, o, -sign, group)
         for i, spot in enumerate(SPOTS):
             for sign in (1, -1):
-                self.cross("xp", sign, i, spot, 0)
+                self.cross("xp", sign, i, spot, 0, "x" + "abc"[i // 5])
             sign = 1 if i % 2 == 0 else -1
-            self.cross("xf", sign, i, spot, 1)
+            self.cross("xf", sign, i, spot, 1, "xd")
 
     def place(self, o1, o2):
         c = self.c
@@ -86,118 +91,106 @@
         return yy * 4 + zz
 
     def tile(self, q):
-        return pl.ds(aligned(DIRECT + TILE * ((self.x + (q + 4)) % 4), TILE), TILE)
-
-    def make(self, src, land, dev, key):
-        k = self.next
-        self.next += 1
-        out = pltpu.make_async_remote_copy(src, src, self.sends.at[k], self.recvs.at[k], device_id=dev, device_id_type=MESH)
-        back = pltpu.make_async_remote_copy(land, land, self.sends.at[k], self.recvs.at[k], device_id=dev, device_id_type=MESH)
-        self.m[key] = (out, back)
-        self.all.append(out)
-
-    def ring(self, kind, sign, which, o1, o2, lo=0, hi=DIRECT):
+        return pl.ds(aligned(self.direct + self.rows * ((self.x + (q + 4)) % 4), 16), self.rows)
+
+    def arrival(self, group):
+        return self.recvs.at[self.number * len(NAMES) + NAMES.index(group)]
+
+    def ring(self, kind, sign, which, o1, o2, group, lo=0, hi=None):
         c = self.c
         along_y = 1 - c if which == 0 else c
         dev = (self.x, (self.y + (sign * along_y + 4)) % 4, (self.z + (sign * (1 - along_y) + 4)) % 4, c)
-        rows = pl.ds(lo, hi - lo) if kind[0] == "d" else self.tile(0)
-        r1, r2 = (o1 - sign, o2) if which == 0 else (o1, o2 - sign)
-        self.make(self.w.at[self.place(o1, o2), rows, :], self.w.at[self.place(r1, r2), rows, :], dev, (kind, sign, o1))
-
-    def cross(self, kind, sign, i, spot, away):
+        rows = pl.ds(lo, (hi or self.direct) - lo) if kind[0] == "d" else self.tile(0)
+        src = self.w.at[self.place(o1, o2), rows, :]
+        self.m[kind, sign, o1] = (src, dev, self.arrival(kind[0] + group))
+
+    def cross(self, kind, sign, i, spot, away, group):
         dev = ((self.x + (sign + 4)) % 4, self.y, self.z, self.c)
-        at = self.place(*spot)
-        src, land = self.w.at[at, self.tile(-sign * away), :], self.w.at[at, self.tile(-sign * (away + 1)), :]
-        self.make(src, land, dev, (kind, sign, i))
+        src = self.w.at[self.place(*spot), self.tile(-sign * away), :]
+        self.m[kind, sign, i] = (src, dev, self.arrival(group))
 
     def go(self, kind, sign, o):
-        self.m[kind, sign, o][0].start()
-
-    def got(self, kind, sign, o):
-        self.m[kind, sign, o][1].wait_recv()
+        src, dev, arrival = self.m[kind, sign, o]
+        pltpu.make_async_remote_copy(src, src, self.sent, arrival, device_id=dev, device_id_type=MESH).start()
+
+    def got(self, group):
+        chips, rows = GROUPS[group], self.direct if group[0] == "d" else self.rows
+        land = self.w.at[pl.ds(0, chips), pl.ds(0, rows), :]
+        me = (self.x, self.y, self.z, 1 - self.c)
+        pltpu.make_async_remote_copy(land, land, self.sent, self.arrival(group), device_id=me, device_id_type=MESH).wait_recv()
 
     def both(self, kind, o):
         self.go(kind, 1, o)
         self.go(kind, -1, o)
 
     def spread(self, *spots):
-        for spot in spots:
-            self.both("xp", SPOTS.index(spot))
+        if self.eager:
+            for spot in spots:
+                self.both("xp", SPOTS.index(spot))
+
+    def sp(self):
+        for i in range(len(SPOTS)):
+            self.both("xp", i)
 
     def qb(self):
         self.both("qp1", 0)
         self.both("qp2", 0)
 
     def q0(self):
-        self.got("qp1", 1, 0)
-        self.go("qf1", 1, -1)
+        self.got("q0")
+        if self.turn == 1:
+            self.go("qf1", 1, -1)
         self.both("qp2", -1)
         self.spread((-1, 0))
 
     def q1(self):
-        self.got("qp1", -1, 0)
+        self.got("q1")
+        if self.turn == -1:
+            self.go("qf1", -1, 1)
         self.both("qp2", 1)
         self.spread((1, 0))
 
     def q2(self):
-        self.got("qp2", 1, 0)
+        self.got("q2")
         self.go("qf2", 1, 0)
-        self.spread((0, -1))
-        self.got("qp2", -1, 0)
-        self.spread((0, 1))
+        self.spread((0, -1), (0, 1))
 
     def q3(self):
-        self.got("qf1", 1, -1)
+        self.got("q3")
         self.both("qp2", 2)
         self.spread((2, 0))
 
     def q4(self):
-        self.got("qp2", 1, -1)
-        self.spread((-1, -1))
-        self.got("qp2", -1, -1)
+        self.got("q4")
         self.go("qf2", -1, -1)
-        self.spread((-1, 1))
-        self.got("qp2", 1, 1)
-        self.spread((1, -1))
-        self.got("qp2", -1, 1)
         self.go("qf2", -1, 1)
-        self.spread((1, 1))
+        self.spread((-1, -1), (-1, 1), (1, -1), (1, 1))
 
     def q5(self):
-        self.got("qf2", 1, 0)
-        self.spread((0, 2))
-        self.got("qp2", 1, 2)
+        self.got("q5")
         self.go("qf2", 1, 2)
-        self.spread((2, -1))
-        self.got("qp2", -1, 2)
-        self.spread((2, 1))
+        self.spread((0, 2), (2, -1), (2, 1))
 
     def q6(self):
-        self.got("qf2", -1, -1)
-        self.spread((-1, 2))
-        self.got("qf2", -1, 1)
-        self.spread((1, 2))
-        self.got("qf2", 1, 2)
-        self.spread((2, 2))
-
-    def x_some(self, lo, hi):
+        self.got("q6")
+        self.spread((-1, 2), (1, 2), (2, 2))
+
+    def x_some(self, group, lo, hi):
+        self.got(group)
         for i in range(lo, hi):
-            for sign in (1, -1):
-                self.got("xp", sign, i)
             self.go("xf", 1 if i % 2 == 0 else -1, i)
 
     def xa(self):
-        self.x_some(0, 5)
+        self.x_some("xa", 0, 5)
 
     def xb(self):
-        self.x_some(5, 10)
+        self.x_some("xb", 5, 10)
 
     def xc(self):
-        self.x_some(10, 15)
+        self.x_some("xc", 10, 15)
 
     def xd(self):
-        for i in range(15):
-            self.got("xf", 1 if i % 2 == 0 else -1, i)
+        self.got("xd")
 
     def db(self):
         self.both("dp1", 0)
@@ -206,49 +199,42 @@
         self.both("dp2", 0)
 
     def d0(self):
-        self.got("dp1", 1, 0)
+        self.got("d0")
         self.go("df1", 1, -1)
         self.both("dp2", -1)
 
     def d1(self):
-        self.got("dp1", -1, 0)
+        self.got("d1")
         self.go("df1", -1, 1)
         self.both("dp2", 1)
 
     def d2(self):
-        self.got("dp2", 1, 0)
+        self.got("d2")
         self.go("df2", 1, 0)
-        self.got("dp2", -1, 0)
 
     def d3(self):
-        self.got("df1", 1, -1)
-        self.got("df1", -1, 1)
+        self.got("d3")
         self.both("dp2", 2)
 
     def d4(self):
-        self.got("dp2", 1, -1)
-        self.go("df2", 1, -1)
-        self.got("dp2", -1, -1)
-        self.go("df2", -1, -1)
+        self.got("d4")
+        self.both("df2", -1)
 
     def d5(self):
-        self.got("dp2", 1, 1)
-        self.got("dp2", -1, 1)
+        self.got("d5")
         self.go("df2", -1, 1)
 
     def d6(self):
-        self.got("dp2", 1, 2)
-        self.go("df2", 1, 2)
-        self.got("dp2", -1, 2)
-        self.go("df2", -1, 2)
+        self.got("d6")
+        self.both("df2", 2)
 
     def d7(self):
-        for sign, o in ((1, 0), (-1, 1), (1, -1), (-1, -1), (1, 2), (-1, 2)):
-            self.got("df2", sign, o)
+        self.got("d7")
 
     def drain(self):
-        for out in self.all:
-            out.wait_send()
+        every = self.w.at[pl.ds(0, 15), :, :]
+        me = (self.x, self.y, self.z, 1 - self.c)
+        pltpu.make_async_remote_copy(every, every, self.sent, self.arrival("d0"), device_id=me, device_id_type=MESH).wait_send()
 
 
 def silu(v):
@@ -266,12 +252,11 @@
         item()
 
 
-def steady(now, then):
-    early = [now.q5, now.d0, now.d1, now.xa, now.q6, now.d2, now.d3]
-    if then is None:
-        return early + [now.xb, now.d4, now.d5, now.d6, now.xc, now.d7, now.xd]
-    middle = [then.qb, now.xb, now.d4, now.d5, then.q0, then.q1, then.q2, now.d6, then.db, then.dc]
-    return early + middle + [now.xc, then.q3, then.q4, now.d7, now.xd]
+def steady(now, then, later):
+    flow = [then.db, then.dc, then.xa, now.d4, now.d5, then.xb, now.d6]
+    if later is not None:
+        flow.append(later.sp)
+    return flow + [then.d0, then.d1, then.xc, then.d2, then.d3, now.d7, now.xd]
 
 
 def kernel(
@@ -279,7 +264,7 @@
     w0, w1, w2, w3, tok, wdt, square, small, nt, pre, xc, bc, y, zs, stl, sbuf, rbuf, pbuf, st0, st0f,
     dts, cum, row, e2, tmp, dec, dsk, cs, cr, drow, pfx, xt, xtr, xcs, xcr,
     gs, gr, ss, sss, ssr,
-    local_sem, gsend, grecv, esend, erecv, asend, arecv, csend, crecv, bsend, brecv, xsend, xrecv,
+    local_sem, gsend, grecv, esend, erecv, asend, arecv, xsend, xrecv,
 ):
     x, yy, zz, c = [lax.axis_index(a) for a in AXES]
     plane = yy * 4 + zz
@@ -354,17 +339,23 @@
             gives[k].wait_recv()
 
     where = (x, yy, zz, c)
-    g = [Gather(w, gsend, grecv, k * PER_GATHER, where) for k, w in enumerate((w0, w1, w2, w3))]
+    g = [Gather(w, gsend, grecv, k, where) for k, w in enumerate((w0, w1, w2, w3))]
     ready((0, 5, 1))
     g[0].qb()
-    g[0].db()
+    ready((2,))
+    g[1].qb()
+    ready((3, 4))
+    g[2].qb()
+    g[3].qb()
     base_rows = aligned(HALO + c * TOKENS, 16)
-    gain = pg[...]
 
     def normalize(r, carry):
         v = tok[pl.ds(aligned(r * 32, 32), 32), :].astype(F32)
         mean = jnp.mean(v * v, axis=-1, keepdims=True)
-        nt[pl.ds(aligned(base_rows + r * 32, 16), 32), :] = (v * lax.rsqrt(mean + EPS) * gain).astype(BF16)
+        scale = lax.rsqrt(mean + EPS)
+        for j in range(MODEL // 128):
+            at = slice(j * 128, (j + 1) * 128)
+            nt[pl.ds(aligned(base_rows + r * 32, 16), 32), at] = (v[:, at] * scale * pg[j : j + 1, :]).astype(BF16)
         return carry
 
     load.wait()
@@ -372,10 +363,14 @@
     tok_rows = nt.at[pl.ds(base_rows, TOKENS), :]
     swap = remote(tok_rows, tok_rows, esend.at[6], erecv.at[6], sib)
     swap.start()
-    g[0].q0()
-    g[0].q1()
-    g[0].dc()
-    g[0].q2()
+
+    def tiles(step):
+        for gather in g:
+            getattr(gather, step)()
+
+    tiles("q0")
+    tiles("q1")
+    tiles("q2")
 
     kk = lax.broadcasted_iota(jnp.int32, (2 * STATE, 256), 0) % STATE
     for j in range(HALF // 256):
@@ -387,20 +382,29 @@
         lo = (v - hi.astype(F32)).astype(BF16)
         return jnp.concatenate([hi, lo], axis=1)
 
-    g[0].d0()
-    g[0].d1()
+    tiles("q3")
+    g[0].db()
+    tiles("q4")
+    g[0].dc()
     swap.wait_recv()
     halo_src, halo_dst = nt.at[pl.ds(CHIP_TOKENS, HALO), :], nt.at[pl.ds(0, HALO), :]
     halo = remote(halo_src, halo_dst, esend.at[7], erecv.at[7], chip_dev(after))
     halo.start()
-    for service in (g[0].q3, g[0].q4, g[0].xa, g[0].q5, g[0].d2, g[0].d3, g[0].q6):
-        service()
-    ready((2,))
-    g[1].qb()
+    tiles("q5")
+    g[0].xa()
+    g[0].d0()
+    g[0].d1()
+    tiles("q6")
+    g[0].xb()
+    g[1].sp()
+    g[0].d2()
+    g[0].d3()
+    g[0].xc()
     roll_by = (STATE - HALF_HEADS * c) % STATE
     skip = pltpu.roll(jnp.broadcast_to(small[2:3, :], (8, STATE)), roll_by, 1)
     dsk[...] = dot(halves(skip), e2[...])
-    for service in (g[0].xb, g[0].d4, g[0].d5, g[1].q0, g[1].q1, g[1].q2, g[0].d6, g[1].db, g[1].dc, g[0].xc):
+    flow = steady(g[0], g[1], g[2])
+    for service in flow[:-2]:
         service()
     halo.wait_recv()
 
@@ -408,7 +412,7 @@
     def _():
         nt[0:HALO, :] = jnp.zeros((HALO, MODEL), BF16)
 
-    for service in (g[1].q3, g[1].q4, g[0].d7, g[0].xd):
+    for service in flow[-2:]:
         service()
 
     def project(w, at):
@@ -419,8 +423,8 @@
 
         return body
 
-    def loop(lo, hi, body):
-        return lambda: lax.fori_loop(lo, hi, body, 0)
+    def loop(lo, hi, body, unroll=False):
+        return lambda: lax.fori_loop(lo, hi, body, 0, unroll=unroll)
 
     tri = jnp.where(
         lax.broadcasted_iota(jnp.int32, (CHUNK, CHUNK), 0) >= lax.broadcasted_iota(jnp.int32, (CHUNK, CHUNK), 1), 1.0, 0.0
@@ -438,11 +442,15 @@
         row[i] = (total + jnp.log(dt) * LOG2E).T
         return carry
 
-    totals, totals_in = [], []
-    for o in range(1, 16):
-        q, p = (plane + o) % 16, (plane + (16 - o)) % 16
-        totals.append(remote(cs, cr.at[plane], csend.at[o - 1], crecv.at[o - 1], plane_dev(q)))
-        totals_in.append(remote(cs, cr.at[p], csend.at[o - 1], crecv.at[o - 1], plane_dev(q)))
+    def exchange(src_of, dst, send, recv):
+        out = []
+        for o in range(1, 16):
+            q = (plane + o) % 16
+            out.append(remote(src_of(q), dst.at[plane], send, recv, plane_dev(q)))
+        everything = remote(dst.at[pl.ds(0, 15)], dst.at[pl.ds(0, 15)], send, recv, sib)
+        return out, everything
+
+    totals, totals_all = exchange(lambda q: cs, cr, asend.at[0], arecv.at[0])
 
     def send_totals():
         running = jnp.zeros((1, STATE), F32)
@@ -457,9 +465,9 @@
             copy.start()
         dec[...] = dot(halves(jnp.exp2(-tmp[...])), e2[...])
 
-    def convolve(at, col):
-        taps = [cw[k : k + 1, col] for k in range(4)]
-        offset = cb[0:1, col]
+    def convolve(at, block):
+        taps = [cw[k : k + 1, pl.ds(aligned(block * 128, 128), 128)] for k in range(4)]
+        offset = cb[pl.ds(block, 1), :]
         parts = []
         for r in range(0, CHIP_TOKENS, CHUNK):
             v = offset
@@ -471,12 +479,12 @@
     swap_bc = remote(bc.at[c], bc.at[c], esend.at[8], erecv.at[8], sib)
 
     def conv_bc():
-        for r, part in enumerate(convolve(pl.ds(0, STATE), pl.ds(aligned(2 * HALF + c * STATE, 128), STATE))):
+        for r, part in enumerate(convolve(pl.ds(0, STATE), 2 * HALF // 128 + c)):
             bc[c, r * CHUNK : (r + 1) * CHUNK, :] = part
         swap_bc.start()
 
     def conv_x(j, carry):
-        parts = convolve(pl.ds(aligned(NARROW + j * 128, 128), 128), pl.ds(aligned(c * HALF + j * 128, 128), 128))
+        parts = convolve(pl.ds(aligned(NARROW + j * 128, 128), 128), c * (HALF // 128) + j)
         for r, part in enumerate(parts):
             xc[r * CHUNK : (r + 1) * CHUNK, pl.ds(aligned(j * 128, 128), 128)] = part
         return carry
@@ -494,11 +502,7 @@
 
         return body
 
-    parts_out, parts_in = [], []
-    for o in range(1, 16):
-        q, p = (plane + o) % 16, (plane + (16 - o)) % 16
-        parts_out.append(remote(sbuf.at[q], rbuf.at[plane], asend.at[o - 1], arecv.at[o - 1], plane_dev(q)))
-        parts_in.append(remote(sbuf.at[q], rbuf.at[p], asend.at[o - 1], arecv.at[o - 1], plane_dev(q)))
+    parts_out, parts_all = exchange(lambda q: sbuf.at[q], rbuf, asend.at[1], arecv.at[1])
 
     def send_parts():
         for q in range(16):
@@ -532,27 +536,21 @@
         stl[0] = jnp.zeros((STATE, HALF), F32)
 
     work = [
-        loop(0, 1, project(w0, 0)), loop(0, CHUNKS, steps), send_totals, conv_bc,
-        loop(1, 2, project(w0, 0)), loop(2, 4, project(w0, 0)), zero_states, loop(0, 6, conv_x), swap_bc.wait_recv,
-        loop(0, CHUNKS, states(0, 3)), loop(0, 2, intra(0, 6)), loop(2, CHUNKS, intra(0, 6)),
+        loop(0, 2, project(w0, 0)), loop(0, CHUNKS, steps, True), send_totals, conv_bc,
+        loop(2, 4, project(w0, 0)), zero_states, loop(0, 6, conv_x), swap_bc.wait_recv,
+        loop(0, CHUNKS, states(0, 3), True),
     ]
-    ready((3, 4))
-    interleave(steady(g[1], g[2]), work)
-
-    work = [
-        loop(0, 2, project(w1, 1024)), loop(6, 10, conv_x), loop(0, CHUNKS, states(3, 5)), send_parts,
-        loop(0, 2, intra(6, 10)), loop(2, CHUNKS, intra(6, 10)),
-    ]
-    flow = steady(g[2], g[3])
-    for item in work[:4]:
-        item()
-        flow.pop(0)()
-    interleave(flow, work[4:])
-
-    for copy in totals_in:
-        copy.wait_recv()
-    for copy in parts_in:
-        copy.wait_recv()
+    interleave(steady(g[1], g[2], g[3]), work)
+
+    def run(*items):
+        for item in items:
+            item()
+
+    run(loop(0, 2, project(w1, 1024)), g[2].d4, g[2].d5, loop(6, 10, conv_x))
+    run(g[2].d6, g[3].db, g[3].dc, loop(0, CHUNKS, states(3, 5), True), send_parts, g[3].xa)
+    run(loop(0, 2, intra(0, 10)), g[3].xb, g[3].d0, g[3].d1, loop(2, CHUNKS, intra(0, 10)), g[3].d2, g[3].xc, g[3].d3, g[3].d4)
+    totals_all.wait_recv()
+    parts_all.wait_recv()
     drow[...] = dot(halves(jnp.exp2(-cr[:, 0, :])), e2[...])
 
     def prefix(k, state):
@@ -586,8 +584,7 @@
 
         return body
 
-    flow = steady(g[3], None)
-    interleave(flow[:6], [loop(0, 2, zdot(w2, 0))])
+    run(g[3].d5, g[3].d6, g[2].d7, g[2].xd, loop(0, 2, zdot(w2, 0)))
     for copy in sec_in:
         copy.wait_recv()
     enter = jnp.zeros((8, HALF), F32)
@@ -601,17 +598,12 @@
 
     lax.fori_loop(0, 16, begin_states, enter)
     st0[plane] = pbuf[plane]
-    starts_out, starts_in = [], []
-    for o in range(1, 16):
-        q, p = (plane + o) % 16, (plane + (16 - o)) % 16
-        starts_out.append(remote(pbuf.at[q], st0.at[plane], bsend.at[o - 1], brecv.at[o - 1], plane_dev(q)))
-        starts_in.append(remote(pbuf.at[q], st0.at[p], bsend.at[o - 1], brecv.at[o - 1], plane_dev(q)))
+    starts_out, starts_all = exchange(lambda q: pbuf.at[q], st0, asend.at[2], arecv.at[2])
     for copy in starts_out:
         copy.start()
-    interleave(flow[6:], [loop(2, 3, zdot(w2, 0))])
+    run(loop(2, 3, zdot(w2, 0)), g[3].d7, g[3].xd)
     lax.fori_loop(0, 2, zdot(w3, 768), 0)
-    for copy in starts_in:
-        copy.wait_recv()
+    starts_all.wait_recv()
     for k in range(16):
         st0f[k * 8 : (k + 1) * 8, :] = st0[k].astype(F32)
 
@@ -650,28 +642,29 @@
     mean = jnp.sum(ss[...] + ssr[...], axis=-1, keepdims=True) * (1.0 / MODEL)
     scale = lax.rsqrt(mean + EPS)
     ours = pl.ds(aligned(c * TOKENS, TOKENS), TOKENS)
-    for j in range(HALF // 256):
-        at = slice(j * 256, (j + 1) * 256)
-        spot = half(c, j * 256, 256)
-        out[:, spot] = (y[ours, at] * scale * ng[0:1, spot]).astype(BF16)
-        spot = half(1 - c, j * 256, 256)
-        out[:, spot] = (gr[:, at].astype(F32) * scale * ng[0:1, spot]).astype(BF16)
+    for j in range(HALF // 128):
+        at = slice(j * 128, (j + 1) * 128)
+        gain = ng[pl.ds(c * (HALF // 128) + j, 1), :]
+        out[:, half(c, j * 128, 128)] = (y[ours, at] * scale * gain).astype(BF16)
+        gain = ng[pl.ds((1 - c) * (HALF // 128) + j, 1), :]
+        out[:, half(1 - c, j * 128, 128)] = (gr[:, at].astype(F32) * scale * gain).astype(BF16)
 
     for gather in g:
         gather.drain()
-    for copy in gives + [swap, halo, swap_bc] + totals + parts_out + sec_out + starts_out + swaps:
+    for copy in gives + [swap, halo, swap_bc, totals_all, parts_all, starts_all] + sec_out + swaps:
         copy.wait_send()
 
 
 def per_device(
     tokens, pre_gain, w_z, w_x, w_bc, w_dt, conv_weight, conv_bias, dt_bias, a_log, d_skip, norm_gain
 ):
-    lines = [v.reshape(1, -1) for v in (conv_bias, pre_gain, norm_gain, dt_bias, a_log, d_skip)]
+    lines = [v.reshape(-1, 128) for v in (conv_bias, pre_gain, norm_gain)]
+    lines += [v.reshape(1, -1) for v in (dt_bias, a_log, d_skip)]
     vmem, anywhere = pl.BlockSpec(memory_space=pltpu.VMEM), pl.BlockSpec(memory_space=pl.ANY)
     dma = pltpu.SemaphoreType.DMA
     return pl.pallas_call(
         kernel,
-        out_shape=jax.ShapeDtypeStruct((TOKENS, MODEL), BF16),
+        out_shape=pltpu.VMEM((TOKENS, MODEL), BF16),
         in_specs=[anywhere] + [vmem] * 7 + [anywhere] * 3 + [vmem],
         out_specs=vmem,
         scratch_shapes=[pltpu.VMEM((16, 2 * SHARD, n), BF16) for n in WIDTHS]
@@ -713,16 +706,12 @@
             pltpu.VMEM((TOKENS, 128), F32),
             pltpu.VMEM((TOKENS, 128), F32),
             dma((7,)),
-            dma((N_GATHER,)),
-            dma((N_GATHER,)),
+            dma((4,)),
+            dma((4 * len(NAMES),)),
             dma((N_EDGE,)),
             dma((N_EDGE,)),
-            dma((15,)),
-            dma((15,)),
-            dma((15,)),
-            dma((15,)),
-            dma((15,)),
-            dma((15,)),
+            dma((3,)),
+            dma((3,)),
             dma((6,)),
             dma((6,)),
         ],

time: 116 us -> 86.6 us (0.75)
  Pallas kernels: 109 us -> 85.4 us
  local copies, waits for them, and re-layouts: 6.39 us -> 1.06 us
    pallas_call x1, Pallas kernels: 109 us -> 85.4 us  [per_device(): pl.pallas_call(kernel, out_shape=pltpu.VMEM((TOKENS, MODEL), BF16), in_sp...]
    reshape x3 -> x0, local copies, waits for them, and re-layouts: 3.93 us -> none  [per_device(): v.reshape(1, -1)]
    unnamed x1, local copies, waits for them, and re-layouts: 2.46 us -> 1.06 us
where the time goes in v3:
time: 86.6 us; the launch traced here: 86.4 us
  Pallas kernels  85.4 us (99%)
  local copies, waits for them, and re-layouts  1.06 us (1%)
    pallas_call x1, Pallas kernels, per_device(): pl.pallas_call(kernel, out_shape=pltpu.VMEM((TOKENS, MODEL), BF16), in_sp...  85.4 us

profile of v3, /device:TPU:1, one launch (start us, length us, event | category | flops | bytes accessed | tf_op | source)
XLA Modules:
  0.0 86.4 jit_solution(15174263375431173357)
XLA Ops:
  0.0 85.4 %shard_map.118 = bf16[256,2560]{1,0:T(8,128)(2,1)S(1)} custom-call(bf16[256,2560]{1,0:T(8,128)(2,1)} %tok_hbm.1, f32[4,2816]{1,0:T(4,128)} %cw.1, f32[22,128]{1,0:T(8,128)} %bitcast.7, f32[20,128]{1,0:T(8,128)} %bitcast.8, f32[20,128]{1,0:T(8,128)} %bitcast.9, f32[1,40]{1,0:T(1,128)} %bitcast.11, f32[1,40]{1,0:T(1,128)} %bitcast.12, f32[1,40]{1,0:T(1,128)} %bitcast.13, ...), custom_call_target="tpu_custom_call" | custom-call | tf_op jit(solution)/shard_map/pallas_call | solution.py:665
  85.4 1.1 %copy.14 = bf16[256,2560]{1,0:T(8,128)(2,1)} copy(bf16[256,2560]{1,0:T(8,128)(2,1)S(1)} %shard_map.118) | data formatting | bytes 2621440
